TPU v7x, 32 devices: a whole 2x2x4 slice. The times are simulated.
32 devices in a mesh: tm: 4 (over x, core), rows: 8 (over z, y).
Axes of the slice: x: 2, y: 2, z: 4, core: 2. Of those that a mesh axis runs over, the one named last changes fastest.
Arguments:
- features: bfloat16 [8, 16, 128, 384], P('tm', 'rows'), may hold values from -6 to 6
- block_gain: float32 [384], replicated, may hold values from 0.5 to 1.5
- conv_weight: bfloat16 [3, 3, 3, 384, 384], replicated, may hold values from -0.0625 to 0.0625
- conv_bias: float32 [384], replicated, may hold values from -3 to 3
- latent_weight: bfloat16 [384, 16], replicated, may hold values from -0.3125 to 0.3125
- latent_bias: float32 [16], replicated, may hold values from -3 to 3
- patch_weight: bfloat16 [64, 5120], replicated, may hold values from -0.75 to 0.75
- patch_bias: float32 [5120], replicated, may hold values from -3 to 3
- shift_mod: float32 [5120], replicated, may hold values from -4 to 4
- scale_mod: float32 [5120], replicated, may hold values from -2 to 2
- query_weight: bfloat16 [5120, 5120], P(None, 'tm'), may hold values from -0.078125 to 0.078125
- query_bias: float32 [5120], P('tm'), may hold values from -4 to 4
- query_gain: float32 [5120], P('tm'), may hold values from 0.5 to 1.5
- key_weight: bfloat16 [5120, 5120], P(None, 'tm'), may hold values from -0.078125 to 0.078125
- key_bias: float32 [5120], P('tm'), may hold values from -4 to 4
- key_gain: float32 [5120], P('tm'), may hold values from 0.5 to 1.5
- packing: int32 [32], replicated, may hold values from 0 to 31, each once
Outputs:
- queries: bfloat16 [4096, 5120], P('rows', 'tm')
- keys: bfloat16 [4096, 5120], P('rows', 'tm')
All inputs are finite; a program needn't handle non-finite values.
Results may differ from a plain program's by a relative error of at most 0.0054.
Values may be sent and summed in bfloat16 or wider, within the bound.
A program may use at most 128 MiB of HBM per device.

v0:
```python
import functools

import jax
import jax.numpy as jnp
from jax import lax
from jax.experimental import pallas as pl
from jax.experimental.pallas import tpu as pltpu
from jax.sharding import PartitionSpec as P

epsilon = 1e-06
MESH = pl.DeviceIdType.MESH
F32, BF16 = jnp.float32, jnp.bfloat16
HIGH = lax.Precision.HIGHEST


def dot(a, b, **kw):
    return jnp.dot(a, b, preferred_element_type=F32, **kw)


def kernel(
    count_t, count_r,
    packing, feat_h, gain_h, conv_h, cbias_h, lw_h, lbias_h, pw_h, pb_h, shift_h, scale_h,
    wq_h, qb_h, wk_h, kb_h,
    q_out, k_out, inv_out,
    feat, gain, conv, cbias, lw, lbias, pw, pb, shift, scale, wq, qb, wk, kb,
    rb, km, lhs, y_ref, fold, snd, rcv, tot, lat_all, emb, mod, tiles, sq, sums_s, sums_r,
    lsem, wsem, hs_sem, hr_sem, as_sem, ar_sem, ss_sem, sr_sem, osem,
):
    t, r = lax.axis_index("tm"), lax.axis_index("rows")
    count = count_t * count_r
    own = t * count_r + r
    _, _, cols, chans = feat.shape
    width = emb.shape[1]
    half = cols // 2
    feats = pw_h.shape[0]
    tokens = mod.shape[0]
    per_block = 2 * half

    small = [(feat_h, feat), (gain_h, gain), (lw_h, lw), (cbias_h, cbias), (lbias_h, lbias)]
    late = [
        (pw_h, pw.at[pl.ds(0, feats)]), (pw_h, pw.at[pl.ds(feats, feats)]), (pb_h, pb), (shift_h, shift),
        (scale_h, scale), (qb_h, qb), (kb_h, kb),
    ]
    copies = [pltpu.make_async_copy(s, d, lsem.at[i]) for i, (s, d) in enumerate(small + late)]
    early, later = copies[: len(small)], copies[len(small) :]
    for c in early:
        c.start()
    conv_copies = [pltpu.make_async_copy(conv_h.at[:, b], conv.at[:, b], wsem.at[b]) for b in range(3)]
    for c in conv_copies:
        c.start()
    for c in later:
        c.start()
    wq_copy = pltpu.make_async_copy(wq_h, wq, wsem.at[3])
    wk_copy = pltpu.make_async_copy(wk_h, wk, wsem.at[4])

    barrier = pltpu.get_barrier_semaphore()

    def greet(i, c):
        other = lax.rem(own + i, count)
        pl.semaphore_signal(barrier, inc=1, device_id=(other // count_r, lax.rem(other, count_r)), device_id_type=MESH)
        return c

    lax.fori_loop(1, count, greet, 0)

    for c in early:
        c.wait()

    lats = lw.shape[0]
    tn = (((0,), (0,)), ((), ()))
    li = lax.broadcasted_iota(jnp.int32, (lats, 2 * feats), 0)
    lj = lax.broadcasted_iota(jnp.int32, (lats, 2 * feats), 1)
    both = ((lj % feats) // 4) == li
    e_both = jnp.where(both, 1.0, 0.0)
    e_low = jnp.where(both & (lj < feats), 1.0, 0.0)
    e_high = jnp.where(both & (lj >= feats), 1.0, 0.0)
    lwv = lw[...]
    lw_low = lax.dot_general(lwv, e_low.astype(BF16), tn, preferred_element_type=F32).astype(BF16)
    lw_high = lax.dot_general(lwv, e_high.astype(BF16), tn, preferred_element_type=F32).astype(BF16)
    lw_both = lax.dot_general(lwv, e_both.astype(BF16), tn, preferred_element_type=F32).astype(BF16)
    span = 2 * feats
    rb[...] = jnp.zeros(rb.shape, BF16)
    rb[pl.ds(0, chans), pl.ds(0, span)] = lw_low
    rb[pl.ds(chans, chans), pl.ds(0, span)] = lw_high
    rb[pl.ds(2 * chans, chans), pl.ds(span, span)] = lw_both
    km[pl.ds(3 * chans, chans), :] = jnp.zeros((chans, km.shape[1]), BF16)
    km[pl.ds(3 * chans, chans), pl.ds(2 * span, span)] = lw_low
    cb8 = jnp.broadcast_to(cbias[...].reshape(1, chans), (8, chans))
    lb8 = jnp.broadcast_to(lbias[...].reshape(1, lats), (8, lats))
    bias8 = dot(cb8, lw_both.astype(F32), precision=HIGH) + dot(lb8, e_both, precision=HIGH)

    gain_v = gain[...].reshape(1, chans)
    row_at = lax.broadcasted_iota(jnp.int32, (cols, chans), 0)
    for f in range(2):
        for w in range(2):
            raw = feat[f, w]
            v = raw.astype(F32)
            sm = jnp.mean(v * v, axis=-1, keepdims=True)
            x = v * lax.rsqrt(sm + epsilon) * gain_v
            act = (x / (1.0 + jnp.exp(-x))).astype(BF16)
            a32 = act.astype(F32)
            prev = jnp.where(row_at == 0, 0.0, pltpu.roll(a32, 1, 0))
            nxt = jnp.where(row_at == cols - 1, 0.0, pltpu.roll(a32, cols - 1, 0))
            at = pl.ds((f * 2 + w) * cols, cols)
            lhs[at, pl.ds(0, chans)] = prev.astype(BF16)
            lhs[at, pl.ds(chans, chans)] = act
            lhs[at, pl.ds(2 * chans, chans)] = nxt.astype(BF16)
            lhs[at, pl.ds(3 * chans, chans)] = raw

    rbv = rb[...]
    for b in range(3):
        conv_copies[b].wait()
        if b == 2:
            wq_copy.start()
            wk_copy.start()
        for e in range(3):
            w3 = jnp.concatenate([conv[2, b, e], conv[1, b, e], conv[0, b, e]], axis=1)
            km[pl.ds(e * chans, chans), pl.ds(b * 2 * span, 2 * span)] = dot(w3, rbv).astype(BF16)
        at = pl.ds(b * 2 * span, 2 * span)
        y_ref[:, at] = dot(lhs[...], km[:, at])

    lane = lax.broadcasted_iota(jnp.int32, (cols, span), 1)
    row = lax.broadcasted_iota(jnp.int32, (cols, span), 0)
    even_row = (lane & 2) == 0
    low = lane < feats
    parity = (lane & 1) == (row & 1)

    def y(f, w, b, z):
        return y_ref[pl.ds((f * 2 + w) * cols, cols), pl.ds(b * 2 * span + z * span, span)]

    def mid(f, z):
        return jnp.where(even_row, y(f, 0, 1, z) + y(f, 1, 2, z), y(f, 0, 0, z) + y(f, 1, 1, z))

    def up(f, z):
        return jnp.where(even_row, 0.0, y(f, 0, 2, z))

    def down(f, z):
        return jnp.where(even_row, y(f, 1, 0, z), 0.0)

    for i, part in enumerate((mid, up, down)):
        x0, x1 = part(0, 0), pltpu.roll(part(1, 0), feats, 1)
        mine = jnp.where(low, x0, x0 + x1)
        after = jnp.where(low, x1 + part(0, 1), part(1, 1))
        fold[i] = jnp.where(parity, mine, 0.0)
        fold[3 + i] = jnp.where(parity, after, 0.0)
    for i in range(6):
        snd[i] = fold[i, pl.ds(0, half, 2), :] + fold[i, pl.ds(1, half, 2), :]

    pl.semaphore_wait(barrier, count - 1)

    has_up, has_down = r > 0, r < count_r - 1
    has_next, has_prev = t < count_t - 1, t > 0
    plan = [
        (1, 0, t, r - 1, has_up, has_down),
        (2, 1, t, r + 1, has_down, has_up),
        (3, 2, t + 1, r, has_next, has_prev),
        (4, 3, t + 1, r - 1, has_next & has_up, has_prev & has_down),
        (5, 4, t + 1, r + 1, has_next & has_down, has_prev & has_up),
    ]
    halo = [
        pltpu.make_async_remote_copy(
            src_ref=snd.at[s], dst_ref=rcv.at[d], send_sem=hs_sem.at[d], recv_sem=hr_sem.at[d],
            device_id=(dt, dr), device_id_type=MESH,
        )
        for s, d, dt, dr, _, _ in plan
    ]
    for copy, (_, _, _, _, sends, _) in zip(halo, plan):
        pl.when(sends)(copy.start)
    tot[...] = snd[0] + bias8[0:1, :]
    for copy, (_, d, _, _, _, gets) in zip(halo, plan):
        def take(copy=copy, d=d):
            copy.wait_recv()
            tot[...] += rcv[d]
        pl.when(gets)(take)
    lat_all[own] = tot[...].astype(BF16)

    side = lax.rem(t, 2)
    mate = t + 1 - 2 * side
    group = count // 2
    place = (t // 2) * count_r + r

    def device(p):
        return (p // count_r) * 2 + side, lax.rem(p, count_r)

    def spread(i):
        dt, dr = device(lax.rem(place + i, group))
        return pltpu.make_async_remote_copy(
            src_ref=lat_all.at[own], dst_ref=lat_all.at[own], send_sem=as_sem.at[i], recv_sem=ar_sem.at[own],
            device_id=(dt, dr), device_id_type=MESH,
        )

    def pass_on(i):
        ft, fr = device(lax.rem(place + group - i, group))
        ident = ft * count_r + fr
        return pltpu.make_async_remote_copy(
            src_ref=lat_all.at[ident], dst_ref=lat_all.at[ident], send_sem=as_sem.at[group + i],
            recv_sem=ar_sem.at[ident], device_id=(mate, r), device_id_type=MESH,
        )

    def from_mate(i):
        ft, fr = device(lax.rem(place + group - i, group))
        ident = (ft + 1 - 2 * side) * count_r + fr
        return pltpu.make_async_remote_copy(
            src_ref=lat_all.at[ident], dst_ref=lat_all.at[ident], send_sem=as_sem.at[group + i],
            recv_sem=ar_sem.at[ident], device_id=(mate, r), device_id_type=MESH,
        )

    def send(i, c):
        spread(i).start()
        return c

    lax.fori_loop(1, group, send, 0)
    pass_on(0).start()
    for c in later:
        c.wait()

    def relay(i, c):
        copy = pass_on(i)
        copy.wait_recv()
        copy.start()
        return c

    lax.fori_loop(1, group, relay, 0)

    def arrive(i, c):
        from_mate(i).wait_recv()
        return c

    lax.fori_loop(0, group, arrive, 0)

    step = 512
    plane = lax.broadcasted_iota(jnp.int32, (half, span), 1)

    def lanes_sum(v):
        out = v[:, 0:128]
        for i in range(1, v.shape[1] // 128):
            out = out + v[:, i * 128 : (i + 1) * 128]
        return out

    def block(j, carry):
        p32 = lat_all[packing[r * count_t + j]].astype(F32)
        left = jnp.concatenate(
            [jnp.where(plane < feats, p32, 0.0), jnp.where(plane < feats, 0.0, p32)], axis=0
        ).astype(BF16)
        total = jnp.zeros((per_block, 128), F32)
        for c in range(0, width, step):
            e = dot(left, pw[:, c : c + step]) + pb[pl.ds(c, step)].reshape(1, step)
            emb[:, c : c + step] = e
            total = total + lanes_sum(e)
        center = jnp.sum(total, axis=1, keepdims=True) / width
        total = jnp.zeros((per_block, 128), F32)
        for c in range(0, width, step):
            d = emb[:, c : c + step] - center
            total = total + lanes_sum(d * d)
        inv = lax.rsqrt(jnp.sum(total, axis=1, keepdims=True) / width + epsilon)
        at = pl.ds(pl.multiple_of(j * per_block, per_block), per_block)
        for c in range(0, width, step):
            gains = 1.0 + scale[pl.ds(c, step)].reshape(1, step)
            moved = shift[pl.ds(c, step)].reshape(1, step)
            mod[at, c : c + step] = ((emb[:, c : c + step] - center) * inv * gains + moved).astype(BF16)
        return carry

    lax.fori_loop(0, count_t, block, 0)

    part = wq.shape[1]
    tile = tiles.shape[2]
    count_n = part // tile

    def out_copy(i, n, dst):
        at = pl.ds(pl.multiple_of(n * tile, tile), tile)
        return pltpu.make_async_copy(tiles.at[lax.rem(i * count_n + n, 2)], dst.at[:, at], osem.at[i, n])

    heads = ((wq_copy, wq, qb, q_out), (wk_copy, wk, kb, k_out))
    for i, (copy, w, bias, dst) in enumerate(heads):
        copy.wait()
        lanes = pl.ds(i * 128, 128)
        sq[:, lanes] = jnp.zeros((tokens, 128), F32)

        def project(n, carry, i=i, w=w, bias=bias, dst=dst, lanes=lanes):
            at = pl.ds(pl.multiple_of(n * tile, tile), tile)
            pl.when(n >= 2)(lambda: out_copy(i, n - 2, dst).wait())
            if i:
                pl.when(n < 2)(lambda: out_copy(0, count_n - 2 + n, heads[0][3]).wait())
            v = dot(mod[...], w[:, at]) + bias[at].reshape(1, tile)
            tiles[lax.rem(i * count_n + n, 2)] = v.astype(BF16)
            sq[:, lanes] += lanes_sum(v * v)
            out_copy(i, n, dst).start()
            return carry

        lax.fori_loop(0, count_n, project, 0)

    pick = lax.broadcasted_iota(jnp.int32, (8, 256), 0) // 4 == lax.broadcasted_iota(jnp.int32, (8, 256), 1) // 128
    nt = (((1,), (1,)), ((), ()))
    sums_s[...] = lax.dot_general(
        jnp.where(pick, 1.0, 0.0), sq[...], nt, precision=HIGH, preferred_element_type=F32
    )
    shares = [
        pltpu.make_async_remote_copy(
            src_ref=sums_s, dst_ref=sums_r.at[i - 1], send_sem=ss_sem.at[i - 1], recv_sem=sr_sem.at[i - 1],
            device_id=(lax.rem(t + i, count_t), r), device_id_type=MESH,
        )
        for i in range(1, count_t)
    ]
    for c in shares:
        c.start()
    sums = sums_s[...]
    for i, c in enumerate(shares):
        c.wait_recv()
        sums = sums + sums_r[i]
    inv = lax.rsqrt(sums / width + epsilon)
    first = lax.broadcasted_iota(jnp.int32, (8, 256), 0)
    lane8 = lax.broadcasted_iota(jnp.int32, (8, 256), 1)
    chosen = jnp.where(first == 4 * (lane8 // 128), 1.0, 0.0)
    inv_out[...] = lax.dot_general(inv, chosen, tn, precision=HIGH, preferred_element_type=F32)
    for n in range(count_n - 2, count_n):
        out_copy(1, n, k_out).wait()

    for copy, (_, _, _, _, sends, _) in zip(halo, plan):
        pl.when(sends)(copy.wait_send)

    def sent(i, c):
        spread(i).wait_send()
        return c

    lax.fori_loop(1, group, sent, 0)

    def passed(i, c):
        pass_on(i).wait_send()
        return c

    lax.fori_loop(0, group, passed, 0)
    for c in shares:
        c.wait_send()


def per_device(
    features, block_gain, conv_weight, conv_bias, latent_weight, latent_bias, patch_weight, patch_bias,
    shift_mod, scale_mod, query_weight, query_bias, query_gain, key_weight, key_bias, key_gain, packing,
):
    count_t, count_r = lax.axis_size("tm"), lax.axis_size("rows")
    count = count_t * count_r
    _, _, cols, chans = features.shape
    feats, width = patch_weight.shape
    part = query_weight.shape[1]
    half = cols // 2
    span = 2 * feats
    tokens = count_t * cols
    tile = 256 if part % 256 == 0 else 128
    V = pltpu.VMEM
    operands = (
        packing, features, block_gain, conv_weight, conv_bias, latent_weight.T, latent_bias, patch_weight, patch_bias,
        shift_mod, scale_mod, query_weight, query_bias, key_weight, key_bias,
    )
    like = lambda a: V(a.shape, a.dtype)
    scratch = [like(a) for a in operands[1:7]]
    scratch += [V((2 * feats, width), BF16), like(patch_bias), like(shift_mod), like(scale_mod)]
    scratch += [like(a) for a in operands[11:]]
    scratch += [
        V((3 * chans, 2 * span), BF16),
        V((4 * chans, 6 * span), BF16),
        V((4 * cols, 4 * chans), BF16),
        V((4 * cols, 6 * span), F32),
        V((6, cols, span), F32),
        V((6, half, span), F32),
        V((5, half, span), F32),
        V((half, span), F32),
        V((count, half, span), BF16),
        V((cols, width), F32),
        V((tokens, width), BF16),
        V((2, tokens, tile), BF16),
        V((tokens, 256), F32),
        V((8, tokens), F32),
        V((count_t - 1, 8, tokens), F32),
    ]
    dma = pltpu.SemaphoreType.DMA
    scratch += [dma((12,)), dma((5,)), dma((5,)), dma((5,)), dma((count,)), dma((count,)), dma((count_t - 1,)), dma((count_t - 1,)), dma((2, part // 128))]
    out = jax.ShapeDtypeStruct((tokens, part), BF16)
    query, key, inv = pl.pallas_call(
        functools.partial(kernel, count_t, count_r),
        out_shape=(out, out, jax.ShapeDtypeStruct((tokens, 256), F32)),
        in_specs=[pl.BlockSpec(memory_space=pltpu.SMEM)] + [pl.BlockSpec(memory_space=pl.ANY)] * 14,
        out_specs=(pl.BlockSpec(memory_space=pl.ANY),) * 2 + (pl.BlockSpec(memory_space=V),),
        scratch_shapes=scratch,
        compiler_params=pltpu.CompilerParams(collective_id=0, has_side_effects=True, vmem_limit_bytes=67043328),
    )(*operands)
    return finish(query, key, inv, query_gain, key_gain)


def scaled(q_h, k_h, inv, qg, kg, qo_h, ko_h, q, k, qo, ko, in_sem, out_sem):
    chunks, _, part = q.shape[0], q.shape[1], q.shape[2]
    rows = q.shape[1]
    both = ((q_h, q, qg, qo, qo_h), (k_h, k, kg, ko, ko_h))
    loads, stores = [], []
    for c in range(chunks):
        for i, (src, buf, _, obuf, dst) in enumerate(both):
            at = pl.ds(c * rows, rows)
            loads.append(pltpu.make_async_copy(src.at[at], buf.at[c], in_sem.at[i, c]))
            stores.append(pltpu.make_async_copy(obuf.at[c], dst.at[at], out_sem.at[i, c]))
    for copy in loads:
        copy.start()
    for c in range(chunks):
        for i, (_, buf, gain, obuf, _) in enumerate(both):
            loads[2 * c + i].wait()
            factor = inv[pl.ds(c * rows, rows), pl.ds(i * 128, 128)]
            for n in range(0, part, 128):
                at = pl.ds(n, 128)
                obuf[c, :, at] = (buf[c, :, at].astype(F32) * factor * gain[at].reshape(1, 128)).astype(BF16)
            stores[2 * c + i].start()
    for copy in stores:
        copy.wait()


def finish(query, key, inv, query_gain, key_gain):
    tokens, part = query.shape
    chunks = tokens // 128
    out = jax.ShapeDtypeStruct((tokens, part), BF16)
    V, dma = pltpu.VMEM, pltpu.SemaphoreType.DMA
    return pl.pallas_call(
        scaled,
        out_shape=(out, out),
        in_specs=[pl.BlockSpec(memory_space=pl.ANY)] * 2 + [pl.BlockSpec(memory_space=V)] * 3,
        out_specs=(pl.BlockSpec(memory_space=pl.ANY),) * 2,
        scratch_shapes=[
            V((chunks, 128, part), BF16), V((chunks, 128, part), BF16), V((chunks, 128, part), BF16), V((chunks, 128, part), BF16),
            dma((2, chunks)), dma((2, chunks)),
        ],
        compiler_params=pltpu.CompilerParams(vmem_limit_bytes=67043328),
    )(query, key, inv, query_gain, key_gain)


def solution(mesh):
    in_specs = (
        P("tm", "rows", None, None), P(), P(), P(), P(), P(), P(), P(), P(), P(),
        P(None, "tm"), P("tm"), P("tm"), P(None, "tm"), P("tm"), P("tm"), P(),
    )
    out_specs = (P("rows", "tm"), P("rows", "tm"))
    return jax.shard_map(per_device, mesh=mesh, in_specs=in_specs, out_specs=out_specs, check_vma=False)
```

profile of v0, /device:TPU:1, one launch (start us, length us, event | category | flops | bytes accessed | tf_op | source)
XLA Modules:
  0.0 54.8 jit_solution(15542600945074490180)
XLA Ops:
  0.6 50.5 %shard_map.176 = (bf16[512,1280]{1,0:T(8,128)(2,1)}, bf16[512,1280]{1,0:T(8,128)(2,1)}, f32[512,256]{1,0:T(8,128)}) custom-call(s32[32]{0:T(128)} %packing.1, bf16[2,2,128,384]{3,2,1,0:T(8,128)(2,1)} %feat_h.1, f32[384]{0:T(512)} %gain_h.1, bf16[3,3,3,384,384]{4,3,2,1,0:T(8,128)(2,1)} %conv_h.1, f32[384]{0:T(512)} %cbias_h.1, bf16[16,384]{1,0:T(8,128)(2,1)} %bitcast.1, ...), custom_call_target="tpu_custom_call" | custom-call | tf_op jit(solution)/shard_map/pallas_call | solution.py:377
  51.1 3.7 %shard_map.177 = (bf16[512,1280]{1,0:T(8,128)(2,1)}, bf16[512,1280]{1,0:T(8,128)(2,1)}) custom-call(bf16[512,1280]{1,0:T(8,128)(2,1)} %get-tuple-element.5.q_h, bf16[512,1280]{1,0:T(8,128)(2,1)} %get-tuple-element.6.k_h, f32[512,256]{1,0:T(8,128)} %get-tuple-element.7.inv, f32[1280]{0:T(1024)} %qg.1, f32[1280]{0:T(1024)} %kg.1), custom_call_target="tpu_custom_call" | custom-call | tf_op jit(solution)/shard_map/pallas_call | solution.py:417
where the time goes:
time: 55.4 us; the launch traced here: 54.8 us
  Pallas kernels  54.2 us (98%)
  between operations  0.64 us (1%)
    pallas_call x1, Pallas kernels, per_device(): pl.pallas_call(functools.partial(kernel, count_t, count_r), out_shape=(ou...  50.5 us
    pallas_call x1, Pallas kernels, finish(): pl.pallas_call(scaled, out_shape=(out, out), in_specs=[pl.BlockSpec(memor...  3.74 us

commit v1 on v0

v1 whole, which is shorter than its diff:
```python
import functools

import jax
import jax.numpy as jnp
from jax import lax
from jax.experimental import pallas as pl
from jax.experimental.pallas import tpu as pltpu
from jax.sharding import PartitionSpec as P

epsilon = 1e-06
MESH = pl.DeviceIdType.MESH
F32, BF16 = jnp.float32, jnp.bfloat16
HIGH = lax.Precision.HIGHEST


def dot(a, b, **kw):
    return jnp.dot(a, b, preferred_element_type=F32, **kw)


def split(v):
    hi = v.astype(BF16)
    return hi, (v - hi.astype(F32)).astype(BF16)


def kernel(
    count_t, count_r,
    packing, feat_h, gain_h, conv_h, cbias_h, lw_h, lbias_h, pw_h, pb_h, shift_h, scale_h,
    wq_h, qb_h, qg_h, wk_h, kb_h, kg_h,
    x_out, mat, vec, gram_out,
    feat, gain, conv, cbias, lw, lbias, pw, pb, shift, scale, wq, qb, qg, wk, kb, kg,
    rb, km, lhs, y_ref, fold, snd, rcv, tot, lat_all, mod, cen, m_all, gram_s, gram_r,
    lsem, wsem, hs_sem, hr_sem, as_sem, ar_sem, ss_sem, sr_sem,
):
    t, r = lax.axis_index("tm"), lax.axis_index("rows")
    count = count_t * count_r
    own = t * count_r + r
    _, _, cols, chans = feat.shape
    feats, width = pw.shape
    half = cols // 2

    small = [(feat_h, feat), (gain_h, gain), (lw_h, lw), (cbias_h, cbias), (lbias_h, lbias)]
    late = [
        (pw_h, pw), (pb_h, pb), (shift_h, shift), (scale_h, scale), (qb_h, qb), (kb_h, kb), (qg_h, qg), (kg_h, kg),
    ]
    copies = [pltpu.make_async_copy(s, d, lsem.at[i]) for i, (s, d) in enumerate(small + late)]
    early, later = copies[: len(small)], copies[len(small) :]
    for c in early + later:
        c.start()
    conv_copies = [pltpu.make_async_copy(conv_h.at[:, b], conv.at[:, b], wsem.at[b]) for b in range(3)]
    for c in conv_copies:
        c.start()
    wq_copy = pltpu.make_async_copy(wq_h, wq, wsem.at[3])
    wk_copy = pltpu.make_async_copy(wk_h, wk, wsem.at[4])

    barrier = pltpu.get_barrier_semaphore()

    def greet(i, c):
        other = lax.rem(own + i, count)
        pl.semaphore_signal(barrier, inc=1, device_id=(other // count_r, lax.rem(other, count_r)), device_id_type=MESH)
        return c

    lax.fori_loop(1, count, greet, 0)

    for c in early:
        c.wait()

    def lanes_sum(v):
        out = v[:, 0:128]
        for i in range(1, v.shape[1] // 128):
            out = out + v[:, i * 128 : (i + 1) * 128]
        return out

    lats = lw.shape[0]
    tn = (((0,), (0,)), ((), ()))
    li = lax.broadcasted_iota(jnp.int32, (lats, 2 * feats), 0)
    lj = lax.broadcasted_iota(jnp.int32, (lats, 2 * feats), 1)
    both = ((lj % feats) // 4) == li
    e_both = jnp.where(both, 1.0, 0.0)
    e_low = jnp.where(both & (lj < feats), 1.0, 0.0)
    e_high = jnp.where(both & (lj >= feats), 1.0, 0.0)
    lwv = lw[...]
    lw_low = lax.dot_general(lwv, e_low.astype(BF16), tn, preferred_element_type=F32).astype(BF16)
    lw_high = lax.dot_general(lwv, e_high.astype(BF16), tn, preferred_element_type=F32).astype(BF16)
    lw_both = lax.dot_general(lwv, e_both.astype(BF16), tn, preferred_element_type=F32).astype(BF16)
    span = 2 * feats
    rb[...] = jnp.zeros(rb.shape, BF16)
    rb[pl.ds(0, chans), pl.ds(0, span)] = lw_low
    rb[pl.ds(chans, chans), pl.ds(0, span)] = lw_high
    rb[pl.ds(2 * chans, chans), pl.ds(span, span)] = lw_both
    km[pl.ds(3 * chans, chans), :] = jnp.zeros((chans, km.shape[1]), BF16)
    km[pl.ds(3 * chans, chans), pl.ds(2 * span, span)] = lw_low
    cb8 = jnp.broadcast_to(cbias[...].reshape(1, chans), (8, chans))
    lb8 = jnp.broadcast_to(lbias[...].reshape(1, lats), (8, lats))
    bias8 = dot(cb8, lw_both.astype(F32), precision=HIGH) + dot(lb8, e_both, precision=HIGH)

    gain_v = gain[...].reshape(1, chans)
    row_at = lax.broadcasted_iota(jnp.int32, (cols, chans), 0)
    for f in range(2):
        for w in range(2):
            raw = feat[f, w]
            v = raw.astype(F32)
            sm = jnp.mean(v * v, axis=-1, keepdims=True)
            x = v * lax.rsqrt(sm + epsilon) * gain_v
            act = (x / (1.0 + jnp.exp(-x))).astype(BF16)
            a32 = act.astype(F32)
            prev = jnp.where(row_at == 0, 0.0, pltpu.roll(a32, 1, 0))
            nxt = jnp.where(row_at == cols - 1, 0.0, pltpu.roll(a32, cols - 1, 0))
            at = pl.ds((f * 2 + w) * cols, cols)
            lhs[at, pl.ds(0, chans)] = prev.astype(BF16)
            lhs[at, pl.ds(chans, chans)] = act
            lhs[at, pl.ds(2 * chans, chans)] = nxt.astype(BF16)
            lhs[at, pl.ds(3 * chans, chans)] = raw

    for c in later:
        c.wait()
    rows_m = mod.shape[0] // 2
    step = 512
    total = jnp.zeros((feats, 128), F32)
    total_b = jnp.zeros((1, 128), F32)
    for c in range(0, width, step):
        total = total + lanes_sum(pw[:, c : c + step].astype(F32))
        total_b = total_b + lanes_sum(pb[pl.ds(c, step)].reshape(1, step))
    mean = jnp.sum(total, axis=1, keepdims=True) / width
    mean_b = jnp.sum(total_b, axis=1, keepdims=True) / width
    at16 = lax.broadcasted_iota(jnp.int32, (16, step), 0)
    for c in range(0, width, step):
        gains = 1.0 + scale[pl.ds(c, step)].reshape(1, step)
        center = pw[:, c : c + step].astype(F32) - mean
        center_b = pb[pl.ds(c, step)].reshape(1, step) - mean_b
        moved = shift[pl.ds(c, step)].reshape(1, step)
        last = jnp.where(at16 == 0, center_b * gains, jnp.where(at16 == 1, moved, 0.0))
        for k, part in enumerate(split(center * gains)):
            mod[pl.ds(k * rows_m, feats), c : c + step] = part
        for k, part in enumerate(split(last)):
            mod[pl.ds(k * rows_m + feats, 16), c : c + step] = part
        last = jnp.where(at16 == 0, center_b, 0.0)
        for k, part in enumerate(split(center)):
            cen[pl.ds(k * rows_m, feats), c : c + step] = part
        for k, part in enumerate(split(last)):
            cen[pl.ds(k * rows_m + feats, 16), c : c + step] = part
    nt = (((1,), (1,)), ((), ()))

    def gram_of(v):
        g = lax.dot_general(v, v, nt, preferred_element_type=F32)
        return g[0:rows_m, 0:rows_m] + g[0:rows_m, rows_m:] + g[rows_m:, 0:rows_m] + g[rows_m:, rows_m:]

    gram_s[...] = jnp.zeros(gram_s.shape, F32)
    gram_out[...] = jnp.zeros(gram_out.shape, F32)
    gram_out[0, :, 0:rows_m] = gram_of(cen[...])

    rbv = rb[...]
    for b in range(3):
        conv_copies[b].wait()
        if b == 1:
            wq_copy.start()
        if b == 2:
            wk_copy.start()
        for e in range(3):
            w3 = jnp.concatenate([conv[2, b, e], conv[1, b, e], conv[0, b, e]], axis=1)
            km[pl.ds(e * chans, chans), pl.ds(b * 2 * span, 2 * span)] = dot(w3, rbv).astype(BF16)
        at = pl.ds(b * 2 * span, 2 * span)
        y_ref[:, at] = dot(lhs[...], km[:, at])

    lane = lax.broadcasted_iota(jnp.int32, (cols, span), 1)
    row = lax.broadcasted_iota(jnp.int32, (cols, span), 0)
    even_row = (lane & 2) == 0
    low = lane < feats
    parity = (lane & 1) == (row & 1)

    def y(f, w, b, z):
        return y_ref[pl.ds((f * 2 + w) * cols, cols), pl.ds(b * 2 * span + z * span, span)]

    def mid(f, z):
        return jnp.where(even_row, y(f, 0, 1, z) + y(f, 1, 2, z), y(f, 0, 0, z) + y(f, 1, 1, z))

    def up(f, z):
        return jnp.where(even_row, 0.0, y(f, 0, 2, z))

    def down(f, z):
        return jnp.where(even_row, y(f, 1, 0, z), 0.0)

    for i, part in enumerate((mid, up, down)):
        x0, x1 = part(0, 0), pltpu.roll(part(1, 0), feats, 1)
        mine = jnp.where(low, x0, x0 + x1)
        after = jnp.where(low, x1 + part(0, 1), part(1, 1))
        fold[i] = jnp.where(parity, mine, 0.0)
        fold[3 + i] = jnp.where(parity, after, 0.0)
    for i in range(6):
        snd[i] = fold[i, pl.ds(0, half, 2), :] + fold[i, pl.ds(1, half, 2), :]

    pl.semaphore_wait(barrier, count - 1)

    has_up, has_down = r > 0, r < count_r - 1
    has_next, has_prev = t < count_t - 1, t > 0
    plan = [
        (1, 0, t, r - 1, has_up, has_down),
        (2, 1, t, r + 1, has_down, has_up),
        (3, 2, t + 1, r, has_next, has_prev),
        (4, 3, t + 1, r - 1, has_next & has_up, has_prev & has_down),
        (5, 4, t + 1, r + 1, has_next & has_down, has_prev & has_up),
    ]
    halo = [
        pltpu.make_async_remote_copy(
            src_ref=snd.at[s], dst_ref=rcv.at[d], send_sem=hs_sem.at[d], recv_sem=hr_sem.at[d],
            device_id=(dt, dr), device_id_type=MESH,
        )
        for s, d, dt, dr, _, _ in plan
    ]
    for copy, (_, _, _, _, sends, _) in zip(halo, plan):
        pl.when(sends)(copy.start)
    part = wq.shape[1]
    tile = 256 if part % 256 == 0 else 128
    at_row = lax.broadcasted_iota(jnp.int32, (rows_m, tile), 0)
    heads = ((wq_copy, wq, qb, qg), (wk_copy, wk, kb, kg))

    def project(i):
        copy, w, bias, scaler = heads[i]
        copy.wait()

        def one(n, carry):
            at = pl.ds(pl.multiple_of(n * tile, tile), tile)
            to = pl.ds(pl.multiple_of(i * part + n * tile, 128), tile)
            v = dot(mod[...], w[:, at])
            v = v[0:rows_m] + v[rows_m:] + jnp.where(at_row == feats + 1, bias[at].reshape(1, tile), 0.0)
            for k, piece in enumerate(split(v)):
                m_all[pl.ds(k * rows_m, rows_m), at] = piece
            v = v * scaler[at].reshape(1, tile)
            hi, lo = split(v[0:feats])
            mat[pl.ds(0, feats), to] = hi
            mat[pl.ds(feats, feats), to] = hi
            mat[pl.ds(2 * feats, feats), to] = lo
            mat[pl.ds(3 * feats, feats), to] = lo
            vec[:, to] = v[feats : feats + 8]
            return carry

        lax.fori_loop(0, part // tile, one, 0)
        gram_s[i, :, 0:rows_m] = gram_of(m_all[...])

    project(0)
    tot[...] = snd[0] + bias8[0:1, :]
    for copy, (_, d, _, _, _, gets) in zip(halo, plan):
        def take(copy=copy, d=d):
            copy.wait_recv()
            tot[...] += rcv[d]
        pl.when(gets)(take)
    lat_all[own] = tot[...].astype(BF16)

    side = lax.rem(t, 2)
    mate = t + 1 - 2 * side
    group = count // 2
    place = (t // 2) * count_r + r

    def device(p):
        return (p // count_r) * 2 + side, lax.rem(p, count_r)

    def spread(i):
        dt, dr = device(lax.rem(place + i, group))
        return pltpu.make_async_remote_copy(
            src_ref=lat_all.at[own], dst_ref=lat_all.at[own], send_sem=as_sem.at[i], recv_sem=ar_sem.at[own],
            device_id=(dt, dr), device_id_type=MESH,
        )

    def pass_on(i):
        ft, fr = device(lax.rem(place + group - i, group))
        ident = ft * count_r + fr
        return pltpu.make_async_remote_copy(
            src_ref=lat_all.at[ident], dst_ref=lat_all.at[ident], send_sem=as_sem.at[group + i],
            recv_sem=ar_sem.at[ident], device_id=(mate, r), device_id_type=MESH,
        )

    def from_mate(i):
        ft, fr = device(lax.rem(place + group - i, group))
        ident = (ft + 1 - 2 * side) * count_r + fr
        return pltpu.make_async_remote_copy(
            src_ref=lat_all.at[ident], dst_ref=lat_all.at[ident], send_sem=as_sem.at[group + i],
            recv_sem=ar_sem.at[ident], device_id=(mate, r), device_id_type=MESH,
        )

    def send(i, c):
        spread(i).start()
        return c

    lax.fori_loop(1, group, send, 0)
    pass_on(0).start()
    project(1)
    shares = [
        pltpu.make_async_remote_copy(
            src_ref=gram_s, dst_ref=gram_r.at[i - 1], send_sem=ss_sem.at[i - 1], recv_sem=sr_sem.at[i - 1],
            device_id=(lax.rem(t + i, count_t), r), device_id_type=MESH,
        )
        for i in range(1, count_t)
    ]
    for c in shares:
        c.start()

    def relay(i, c):
        copy = pass_on(i)
        copy.wait_recv()
        copy.start()
        return c

    lax.fori_loop(1, group, relay, 0)

    def arrive(i, c):
        from_mate(i).wait_recv()
        return c

    lax.fori_loop(0, group, arrive, 0)

    for i in range(2):
        gram_out[1 + i] = gram_s[i]
    for i, c in enumerate(shares):
        c.wait_recv()
        for h in range(2):
            gram_out[1 + h] += gram_r[i, h]

    def pick(j, carry):
        x_out[j] = lat_all[packing[r * count_t + j]]
        return carry

    lax.fori_loop(0, count_t, pick, 0)

    for copy, (_, _, _, _, sends, _) in zip(halo, plan):
        pl.when(sends)(copy.wait_send)

    def sent(i, c):
        spread(i).wait_send()
        return c

    lax.fori_loop(1, group, sent, 0)

    def passed(i, c):
        pass_on(i).wait_send()
        return c

    lax.fori_loop(0, group, passed, 0)
    for c in shares:
        c.wait_send()


def per_device(
    features, block_gain, conv_weight, conv_bias, latent_weight, latent_bias, patch_weight, patch_bias,
    shift_mod, scale_mod, query_weight, query_bias, query_gain, key_weight, key_bias, key_gain, packing,
):
    count_t, count_r = lax.axis_size("tm"), lax.axis_size("rows")
    count = count_t * count_r
    _, _, cols, chans = features.shape
    feats, width = patch_weight.shape
    part = query_weight.shape[1]
    half = cols // 2
    span = 2 * feats
    V = pltpu.VMEM
    rows_m = feats + 16
    operands = (
        packing, features, block_gain, conv_weight, conv_bias, latent_weight.T, latent_bias, patch_weight, patch_bias,
        shift_mod, scale_mod, query_weight, query_bias, query_gain, key_weight, key_bias, key_gain,
    )
    like = lambda a: V(a.shape, a.dtype)
    scratch = [like(a) for a in operands[1:]]
    scratch += [
        V((3 * chans, 2 * span), BF16),
        V((4 * chans, 6 * span), BF16),
        V((4 * cols, 4 * chans), BF16),
        V((4 * cols, 6 * span), F32),
        V((6, cols, span), F32),
        V((6, half, span), F32),
        V((5, half, span), F32),
        V((half, span), F32),
        V((count, half, span), BF16),
        V((2 * rows_m, width), BF16),
        V((2 * rows_m, width), BF16),
        V((2 * rows_m, part), BF16),
        V((2, rows_m, 128), F32),
        V((count_t - 1, 2, rows_m, 128), F32),
    ]
    dma = pltpu.SemaphoreType.DMA
    scratch += [dma((13,)), dma((5,)), dma((5,)), dma((5,)), dma((count,)), dma((count,)), dma((count_t - 1,)), dma((count_t - 1,))]
    outs = (
        jax.ShapeDtypeStruct((count_t, half, span), BF16),
        jax.ShapeDtypeStruct((4 * feats, 2 * part), BF16),
        jax.ShapeDtypeStruct((8, 2 * part), F32),
        jax.ShapeDtypeStruct((3, rows_m, 128), F32),
    )
    x, mat, vec, gram = pl.pallas_call(
        functools.partial(kernel, count_t, count_r),
        out_shape=outs,
        in_specs=[pl.BlockSpec(memory_space=pltpu.SMEM)] + [pl.BlockSpec(memory_space=pltpu.HBM)] * 16,
        out_specs=(pl.BlockSpec(memory_space=V),) * 4,
        scratch_shapes=scratch,
        compiler_params=pltpu.CompilerParams(collective_id=0, has_side_effects=True, vmem_limit_bytes=50 * 2**20),
    )(*operands)
    return finish(width, x, mat, vec, gram)


def final(width, x_ref, mat, vec, gram, q_h, k_h, left, coef, tiles, osem):
    count_t, half, span = x_ref.shape
    feats = span // 2
    part = mat.shape[1] // 2
    tokens = left.shape[0]
    tile = tiles.shape[2]
    plane = lax.broadcasted_iota(jnp.int32, (half, span), 1)
    for j in range(count_t):
        p32 = x_ref[j].astype(F32)
        low = jnp.where(plane < feats, p32, 0.0).astype(BF16)
        high = jnp.where(plane < feats, 0.0, p32).astype(BF16)
        for k in range(2):
            left[pl.ds(j * 2 * half, half), pl.ds(k * span, span)] = low
            left[pl.ds(j * 2 * half + half, half), pl.ds(k * span, span)] = high
    lane = lax.broadcasted_iota(jnp.int32, (1, span), 1)

    def quad(g):
        rows = g.shape[0]
        lane_g = lax.broadcasted_iota(jnp.int32, (rows, span), 1)
        twice = jnp.where(lane_g < feats, g, pltpu.roll(g, feats, 1))
        hi, lo = split(jnp.concatenate([twice[0:feats], twice[0:feats]], axis=0))
        return jnp.concatenate([hi, lo], axis=0), twice[feats : feats + 1], twice[feats + 1 : feats + 2]

    def entry(row, at):
        return jnp.sum(jnp.where(lane == at, row, 0.0), axis=1, keepdims=True)

    ge, gq, gk = gram[0], gram[1], gram[2]
    quads = [quad(g) for g in (ge, gq, gk)]
    stacked = jnp.concatenate([q[0] for q in quads], axis=1)
    rows = 128
    for c in range(0, tokens, rows):
        at = pl.ds(c, rows)
        y2 = left[at, :]
        prod = dot(y2, stacked)
        y = y2[:, 0:span].astype(F32)
        e = jnp.sum(y * (prod[:, 0:span] + 2.0 * quads[0][1]), axis=1, keepdims=True) + entry(ge[feats : feats + 1], feats)
        inv = lax.rsqrt(e / width + epsilon)
        for i, g in enumerate((gq, gk)):
            body = inv * (prod[:, (1 + i) * span : (2 + i) * span] + 2.0 * quads[1 + i][1]) + 2.0 * quads[1 + i][2]
            ss = inv * jnp.sum(y * body, axis=1, keepdims=True)
            ss = ss + inv * inv * entry(g[feats : feats + 1], feats)
            ss = ss + 2.0 * inv * entry(g[feats : feats + 1], feats + 1) + entry(g[feats + 1 : feats + 2], feats + 1)
            norm = lax.rsqrt(ss / width + epsilon)
            coef[2 * i, at, :] = jnp.broadcast_to(norm * inv, (rows, 128))
            coef[2 * i + 1, at, :] = jnp.broadcast_to(norm, (rows, 128))
    count_n = part // tile

    def out_copy(i, n, dst):
        return pltpu.make_async_copy(tiles.at[i * count_n + n], dst.at[:, pl.ds(n * tile, tile)], osem.at[i, n])

    for i, dst in enumerate((q_h, k_h)):
        for n in range(count_n):
            for c in range(0, tokens, 256):
                at = pl.ds(c, 256)
                v = dot(left[at, :], mat[:, pl.ds(i * part + n * tile, tile)])
                for l in range(0, tile, 128):
                    to = pl.ds(i * part + n * tile + l, 128)
                    o = coef[2 * i, at, :] * (v[:, l : l + 128] + vec[0:1, to]) + coef[2 * i + 1, at, :] * vec[1:2, to]
                    tiles[i * count_n + n, at, pl.ds(l, 128)] = o.astype(BF16)
            out_copy(i, n, dst).start()
    for i, dst in enumerate((q_h, k_h)):
        for n in range(count_n):
            out_copy(i, n, dst).wait()


def finish(width, x, mat, vec, gram):
    count_t, half, span = x.shape
    tokens, part = count_t * 2 * half, mat.shape[1] // 2
    tile = 256 if part % 256 == 0 else 128
    out = jax.ShapeDtypeStruct((tokens, part), BF16)
    V, dma = pltpu.VMEM, pltpu.SemaphoreType.DMA
    return pl.pallas_call(
        functools.partial(final, width),
        out_shape=(out, out),
        in_specs=[pl.BlockSpec(memory_space=V)] * 4,
        out_specs=(pl.BlockSpec(memory_space=pl.ANY),) * 2,
        scratch_shapes=[
            V((tokens, 2 * span), BF16), V((4, tokens, 128), F32), V((2 * part // tile, tokens, tile), BF16),
            dma((2, part // tile)),
        ],
        compiler_params=pltpu.CompilerParams(vmem_limit_bytes=24 * 2**20),
    )(x, mat, vec, gram)


def solution(mesh):
    in_specs = (
        P("tm", "rows", None, None), P(), P(), P(), P(), P(), P(), P(), P(), P(),
        P(None, "tm"), P("tm"), P("tm"), P(None, "tm"), P("tm"), P("tm"), P(),
    )
    out_specs = (P("rows", "tm"), P("rows", "tm"))
    return jax.shard_map(per_device, mesh=mesh, in_specs=in_specs, out_specs=out_specs, check_vma=False)
```

time: 55.4 us -> 40.9 us (0.74)
  Pallas kernels: 54.2 us -> 29.1 us
  local copies, waits for them, and re-layouts: 0 us -> 10.4 us
    pallas_call x2, Pallas kernels: 54.2 us -> 29.1 us  [the longest x1 26.6 us: per_device(): pl.pallas_call(functools.partial(kernel, count_t, count_r), out_shape=out...]
    unnamed x0 -> x28, local copies, waits for them, and re-layouts: none -> 10.4 us
where the time goes in v1:
time: 40.9 us; the launch traced here: 40.2 us
  Pallas kernels  29.1 us (71%)
  local copies, waits for them, and re-layouts  10.4 us (25%)
  between operations  0.67 us (2%)
    pallas_call x1, Pallas kernels, per_device(): pl.pallas_call(functools.partial(kernel, count_t, count_r), out_shape=out...  26.6 us
    unnamed x28, local copies, waits for them, and re-layouts  10.4 us
    pallas_call x1, Pallas kernels, finish(): pl.pallas_call(functools.partial(final, width), out_shape=(out, out), in_...  2.48 us

profile of v1, /device:TPU:1, one launch (start us, length us, event | category | flops | bytes accessed | tf_op | source)
XLA Modules:
  0.0 40.2 jit_solution(7029399246679587638)
XLA Ops:
  0.6 0.0 copy-start
  0.6 1.1 %copy-done = bf16[64,5120]{1,0:T(8,128)(2,1)S(1)} copy-done((bf16[64,5120]{1,0:T(8,128)(2,1)S(1)}, bf16[64,5120]{1,0:T(8,128)(2,1)}, u32[]{:S(2)}) %copy-start) | copy-done | bytes 655384
  1.7 0.0 copy-start.1
  1.7 1.0 %copy-done.1 = bf16[2,2,128,384]{3,2,1,0:T(8,128)(2,1)S(1)} copy-done((bf16[2,2,128,384]{3,2,1,0:T(8,128)(2,1)S(1)}, bf16[2,2,128,384]{3,2,1,0:T(8,128)(2,1)}, u32[]{:S(2)}) %copy-start.1) | copy-done | bytes 393240
  2.7 0.0 copy-start.2
  2.7 0.7 %copy-done.2 = f32[5120]{0:T(1024)S(1)} copy-done((f32[5120]{0:T(1024)S(1)}, f32[5120]{0:T(1024)}, u32[]{:S(2)}) %copy-start.2) | copy-done | bytes 20504
  3.5 0.0 copy-start.3
  3.5 0.7 %copy-done.3 = f32[5120]{0:T(1024)S(1)} copy-done((f32[5120]{0:T(1024)S(1)}, f32[5120]{0:T(1024)}, u32[]{:S(2)}) %copy-start.3) | copy-done | bytes 20504
  4.2 0.0 copy-start.4
  4.2 0.7 %copy-done.4 = f32[5120]{0:T(1024)S(1)} copy-done((f32[5120]{0:T(1024)S(1)}, f32[5120]{0:T(1024)}, u32[]{:S(2)}) %copy-start.4) | copy-done | bytes 20504
  4.9 0.0 copy-start.5
  4.9 0.7 %copy-done.5 = bf16[384,16]{0,1:T(8,128)(2,1)S(1)} copy-done((bf16[384,16]{0,1:T(8,128)(2,1)S(1)}, bf16[384,16]{0,1:T(8,128)(2,1)}, u32[]{:S(2)}) %copy-start.5) | copy-done | bytes 12312
  5.6 0.0 copy-start.6
  5.6 0.7 %copy-done.6 = f32[1280]{0:T(1024)S(1)} copy-done((f32[1280]{0:T(1024)S(1)}, f32[1280]{0:T(1024)}, u32[]{:S(2)}) %copy-start.6) | copy-done | bytes 5144
  6.3 0.0 copy-start.7
  6.3 0.7 %copy-done.7 = f32[1280]{0:T(1024)S(1)} copy-done((f32[1280]{0:T(1024)S(1)}, f32[1280]{0:T(1024)}, u32[]{:S(2)}) %copy-start.7) | copy-done | bytes 5144
  7.0 0.0 copy-start.8
  7.0 0.7 %copy-done.8 = f32[1280]{0:T(1024)S(1)} copy-done((f32[1280]{0:T(1024)S(1)}, f32[1280]{0:T(1024)}, u32[]{:S(2)}) %copy-start.8) | copy-done | bytes 5144
  7.7 0.0 copy-start.9
  7.7 0.7 %copy-done.9 = f32[1280]{0:T(1024)S(1)} copy-done((f32[1280]{0:T(1024)S(1)}, f32[1280]{0:T(1024)}, u32[]{:S(2)}) %copy-start.9) | copy-done | bytes 5144
  8.4 0.0 copy-start.10
  8.4 0.7 %copy-done.10 = f32[384]{0:T(512)S(1)} copy-done((f32[384]{0:T(512)S(1)}, f32[384]{0:T(512)}, u32[]{:S(2)}) %copy-start.10) | copy-done | bytes 1560
  9.1 0.0 copy-start.11
  9.1 0.7 %copy-done.11 = f32[384]{0:T(512)S(1)} copy-done((f32[384]{0:T(512)S(1)}, f32[384]{0:T(512)}, u32[]{:S(2)}) %copy-start.11) | copy-done | bytes 1560
  9.8 0.0 copy-start.12
  9.8 0.7 %copy-done.12 = s32[32]{0:T(128)S(1)} copy-done((s32[32]{0:T(128)S(1)}, s32[32]{0:T(128)}, u32[]{:S(2)}) %copy-start.12) | copy-done | bytes 152
  10.4 0.0 copy-start.13
  10.4 0.7 %copy-done.13 = f32[16]{0:T(128)S(1)} copy-done((f32[16]{0:T(128)S(1)}, f32[16]{0:T(128)}, u32[]{:S(2)}) %copy-start.13) | copy-done | bytes 88
  11.1 26.6 %shard_map.176 = (bf16[4,64,128]{2,1,0:T(8,128)(2,1)S(1)}, bf16[256,2560]{1,0:T(8,128)(2,1)S(1)}, f32[8,2560]{1,0:T(8,128)S(1)}, f32[3,80,128]{2,1,0:T(8,128)S(1)}) custom-call(s32[32]{0:T(128)S(1)} %copy-done.12, bf16[2,2,128,384]{3,2,1,0:T(8,128)(2,1)S(1)} %copy-done.1, f32[384]{0:T(512)S(1)} %copy-done.10, bf16[3,3,3,384,384]{4,3,2,1,0:T(8,128)(2,1)} %conv_h.1, ...), custom_call_target="tpu_custom_call" | custom-call | tf_op jit(solution)/shard_map/pallas_call | solution.py:384
  37.7 2.5 %shard_map.177 = (bf16[512,1280]{1,0:T(8,128)(2,1)}, bf16[512,1280]{1,0:T(8,128)(2,1)}) custom-call(bf16[4,64,128]{2,1,0:T(8,128)(2,1)S(1)} %get-tuple-element.6.x_ref, bf16[256,2560]{1,0:T(8,128)(2,1)S(1)} %get-tuple-element.7.mat, f32[8,2560]{1,0:T(8,128)S(1)} %get-tuple-element.8.vec, f32[3,80,128]{2,1,0:T(8,128)S(1)} %get-tuple-element.9.gram), custom_call_target="tpu_custom_call" | custom-call | tf_op jit(solution)/shard_map/pallas_call | solution.py:466
Async XLA Ops:
  0.6 1.1 %copy-start = (bf16[64,5120]{1,0:T(8,128)(2,1)S(1)}, bf16[64,5120]{1,0:T(8,128)(2,1)}, u32[]{:S(2)}) copy-start(bf16[64,5120]{1,0:T(8,128)(2,1)} %pw_h.1) | copy-start | bytes 1966084
  1.7 1.0 %copy-start.1 = (bf16[2,2,128,384]{3,2,1,0:T(8,128)(2,1)S(1)}, bf16[2,2,128,384]{3,2,1,0:T(8,128)(2,1)}, u32[]{:S(2)}) copy-start(bf16[2,2,128,384]{3,2,1,0:T(8,128)(2,1)} %feat_h.1) | copy-start | bytes 1179652
  2.7 0.7 %copy-start.2 = (f32[5120]{0:T(1024)S(1)}, f32[5120]{0:T(1024)}, u32[]{:S(2)}) copy-start(f32[5120]{0:T(1024)} %pb_h.1) | copy-start | bytes 61444
  3.5 0.7 %copy-start.3 = (f32[5120]{0:T(1024)S(1)}, f32[5120]{0:T(1024)}, u32[]{:S(2)}) copy-start(f32[5120]{0:T(1024)} %shift_h.1) | copy-start | bytes 61444
  4.2 0.7 %copy-start.4 = (f32[5120]{0:T(1024)S(1)}, f32[5120]{0:T(1024)}, u32[]{:S(2)}) copy-start(f32[5120]{0:T(1024)} %scale_h.1) | copy-start | bytes 61444
  4.9 0.7 %copy-start.5 = (bf16[384,16]{0,1:T(8,128)(2,1)S(1)}, bf16[384,16]{0,1:T(8,128)(2,1)}, u32[]{:S(2)}) copy-start(bf16[384,16]{0,1:T(8,128)(2,1)} %param.21) | copy-start | bytes 36868
  5.6 0.7 %copy-start.6 = (f32[1280]{0:T(1024)S(1)}, f32[1280]{0:T(1024)}, u32[]{:S(2)}) copy-start(f32[1280]{0:T(1024)} %qb_h.1) | copy-start | bytes 15364
  6.3 0.7 %copy-start.7 = (f32[1280]{0:T(1024)S(1)}, f32[1280]{0:T(1024)}, u32[]{:S(2)}) copy-start(f32[1280]{0:T(1024)} %qg_h.1) | copy-start | bytes 15364
  7.0 0.7 %copy-start.8 = (f32[1280]{0:T(1024)S(1)}, f32[1280]{0:T(1024)}, u32[]{:S(2)}) copy-start(f32[1280]{0:T(1024)} %kb_h.1) | copy-start | bytes 15364
  7.7 0.7 %copy-start.9 = (f32[1280]{0:T(1024)S(1)}, f32[1280]{0:T(1024)}, u32[]{:S(2)}) copy-start(f32[1280]{0:T(1024)} %kg_h.1) | copy-start | bytes 15364
  8.4 0.7 %copy-start.10 = (f32[384]{0:T(512)S(1)}, f32[384]{0:T(512)}, u32[]{:S(2)}) copy-start(f32[384]{0:T(512)} %gain_h.1) | copy-start | bytes 4612
  9.1 0.7 %copy-start.11 = (f32[384]{0:T(512)S(1)}, f32[384]{0:T(512)}, u32[]{:S(2)}) copy-start(f32[384]{0:T(512)} %cbias_h.1) | copy-start | bytes 4612
  9.8 0.7 %copy-start.12 = (s32[32]{0:T(128)S(1)}, s32[32]{0:T(128)}, u32[]{:S(2)}) copy-start(s32[32]{0:T(128)} %packing.1) | copy-start | bytes 388
  10.4 0.7 %copy-start.13 = (f32[16]{0:T(128)S(1)}, f32[16]{0:T(128)}, u32[]{:S(2)}) copy-start(f32[16]{0:T(128)} %lbias_h.1) | copy-start | bytes 196

commit v2 on v1

v2 whole, which is shorter than its diff:
```python
import functools

import jax
import jax.numpy as jnp
from jax import lax
from jax.experimental import pallas as pl
from jax.experimental.pallas import tpu as pltpu
from jax.sharding import PartitionSpec as P

epsilon = 1e-06
MESH = pl.DeviceIdType.MESH
F32, BF16 = jnp.float32, jnp.bfloat16


def dot(a, b, **kw):
    return jnp.dot(a, b, preferred_element_type=F32, **kw)


def split(v):
    hi = v.astype(BF16)
    return hi, (v - hi.astype(F32)).astype(BF16)


def kernel(
    count_t, count_r,
    packing_h, feat_h, gain_h, conv_h, cbias_h, lw_h, lbias_h, pw_h, pb_h, shift_h, scale_h,
    wq_h, qb_h, qg_h, wk_h, kb_h, kg_h,
    x_out, mat, gram_out,
    packing, feat, gain, conv, cbias, lw, lbias, pw, pb, shift, scale, w_all, qb, kb, qg, kg, rows_qk,
    scr, km, lhs, y_ref, snd, rcv, tot, lat_all, pwf, bounce, mod, cen, m_all, gram, gram_s, gram_r,
    lsem, csem, wsem, hs_sem, hr_sem, as_sem, ar_sem, ss_sem, sr_sem,
):
    t, r = lax.axis_index("tm"), lax.axis_index("rows")
    count = count_t * count_r
    own = t * count_r + r
    _, _, cols, chans = feat.shape
    feats, width = pw.shape
    lats = lw.shape[0]
    half = cols // 2
    part = wq_h.shape[1]
    tile = w_all.shape[2]
    count_n = part // tile
    rows_m = mod.shape[0] // 2

    early = [(feat_h, feat), (gain_h, gain), (lw_h, lw)]
    late = [
        (pw_h, pw), (pb_h, pb), (shift_h, shift), (scale_h, scale), (cbias_h, cbias), (lbias_h, lbias),
        (qb_h, qb), (kb_h, kb), (qg_h, qg), (kg_h, kg), (packing_h, packing),
    ]
    copies = [pltpu.make_async_copy(s, d, lsem.at[i]) for i, (s, d) in enumerate(early + late)]
    first, later = copies[: len(early)], copies[len(early) :]
    taps = [pltpu.make_async_copy(conv_h.at[i // 3, i % 3], conv.at[i // 3, i % 3], csem.at[i]) for i in range(9)]
    for c in first + taps + later:
        c.start()
    loads = [
        pltpu.make_async_copy(w.at[:, pl.ds(n * tile, tile)], w_all.at[h * count_n + n], wsem.at[h * count_n + n])
        for h, w in enumerate((wq_h, wk_h)) for n in range(count_n)
    ]

    barrier = pltpu.get_barrier_semaphore()

    def greet(i, c):
        other = lax.rem(own + i, count)
        pl.semaphore_signal(barrier, inc=1, device_id=(other // count_r, lax.rem(other, count_r)), device_id_type=MESH)
        return c

    lax.fori_loop(1, count, greet, 0)
    nt = (((1,), (1,)), ((), ()))

    for c in first:
        c.wait()
    lwv = lw[...]
    gain_v = gain[...].reshape(1, chans)
    row_at = lax.broadcasted_iota(jnp.int32, (half, 128), 0)
    for f in range(2):
        for w in range(2):
            v = feat[f, w].astype(F32)
            sm = jnp.mean(v * v, axis=-1, keepdims=True)
            x = v * lax.rsqrt(sm + epsilon) * gain_v
            act = (x / (1.0 + jnp.exp(-x))).astype(BF16).astype(F32)
            base = (f * 2 + w) * cols
            for l in range(chans // 128):
                scr[0, l] = act[:, l * 128 : (l + 1) * 128]
                scr[1, l] = v[:, l * 128 : (l + 1) * 128]
                even, odd = scr[0, l, pl.ds(0, half, 2), :], scr[0, l, pl.ds(1, half, 2), :]
                before = jnp.where(row_at == 0, 0.0, pltpu.roll(odd, 1, 0))
                after = jnp.where(row_at == half - 1, 0.0, pltpu.roll(even, half - 1, 0))
                plain = (scr[1, l, pl.ds(0, half, 2), :], scr[1, l, pl.ds(1, half, 2), :])
                for k, (low, high) in enumerate(((before, even), (even, odd), (odd, after), plain)):
                    lhs[pl.ds(base, half), pl.ds(k * chans + l * 128, 128)] = low.astype(BF16)
                    lhs[pl.ds(base + half, half), pl.ds(k * chans + l * 128, 128)] = high.astype(BF16)

    none = jnp.zeros((lats, chans), BF16)
    pair = jnp.concatenate(
        [jnp.concatenate([lwv, none], axis=1), jnp.concatenate([none, lwv], axis=1)], axis=0
    )
    km[:, pl.ds(3 * chans, chans)] = jnp.zeros((9 * lats, chans), BF16)
    km[pl.ds(7 * lats, lats), pl.ds(3 * chans, chans)] = lwv
    started = 0
    for p in range(5):
        ids = [i for i in (2 * p, 2 * p + 1) if i < 9]
        for i in ids:
            taps[i].wait()
        more = min(len(loads), (p + 1) * -(-len(loads) // 5))
        for c in loads[started:more]:
            c.start()
        started = more
        for e in range(3):
            rhs = jnp.concatenate([conv[i // 3, i % 3, e] for i in ids], axis=1)
            left = pair if len(ids) == 2 else lwv
            folded = lax.dot_general(left, rhs, nt, preferred_element_type=F32)
            km[pl.ds(ids[0] * lats, lats * len(ids)), pl.ds(e * chans, chans)] = folded.astype(BF16)
    y_ref[...] = lax.dot_general(km[...], lhs[...], nt, preferred_element_type=F32)

    def total(d, q):
        out = None
        for f in range(2):
            for w in range(2):
                a, b = f + 2 - d, w + 1 - q
                if 0 <= a < 3 and 0 <= b < 3:
                    term = y_ref[pl.ds((a * 3 + b) * lats, lats), pl.ds((f * 2 + w) * cols, cols)]
                    out = term if out is None else out + term
        return out

    sent = [(0, -1), (1, -1), (0, 2), (1, 2), (2, 0), (2, 1), (3, 0), (3, 1), (2, -1), (3, -1), (2, 2), (3, 2)]
    for i, (d, q) in enumerate(sent):
        snd[pl.ds(i * lats, lats), :] = total(d, q)

    pl.semaphore_wait(barrier, count - 1)

    has_up, has_down = r > 0, r < count_r - 1
    has_next, has_prev = t < count_t - 1, t > 0
    plan = [
        (0, 2, t, r - 1, has_up, has_down, (1, 3)),
        (2, 2, t, r + 1, has_down, has_up, (0, 2)),
        (4, 4, t + 1, r, has_next, has_prev, (0, 1, 2, 3)),
        (8, 2, t + 1, r - 1, has_next & has_up, has_prev & has_down, (1, 3)),
        (10, 2, t + 1, r + 1, has_next & has_down, has_prev & has_up, (0, 2)),
    ]
    halo = []
    for k, (at, n, dt, dr, _, _, _) in enumerate(plan):
        rows = pl.ds(at * lats, n * lats)
        halo.append(pltpu.make_async_remote_copy(
            src_ref=snd.at[rows], dst_ref=rcv.at[rows], send_sem=hs_sem.at[k], recv_sem=hr_sem.at[k],
            device_id=(dt, dr), device_id_type=MESH,
        ))
    for copy, p in zip(halo, plan):
        pl.when(p[4])(copy.start)

    for c in later:
        c.wait()
    offset = jnp.sum(lwv.astype(F32) * cbias[...].reshape(1, chans), axis=1, keepdims=True)
    at_l = lax.broadcasted_iota(jnp.int32, (lats, lats), 0) == lax.broadcasted_iota(jnp.int32, (lats, lats), 1)
    offset = offset + jnp.sum(jnp.where(at_l, lbias[...].reshape(1, lats), 0.0), axis=1, keepdims=True)
    for i, (d, q) in enumerate(((0, 0), (0, 1), (1, 0), (1, 1))):
        tot[pl.ds(i * lats, lats), :] = total(d, q) + offset

    step = 512

    def lanes_sum(v):
        out = v[:, 0:128]
        for i in range(1, v.shape[1] // 128):
            out = out + v[:, i * 128 : (i + 1) * 128]
        return out

    total_w = jnp.zeros((feats, 128), F32)
    total_b = jnp.zeros((1, 128), F32)
    groups = feats // lats
    for c in range(0, width, step):
        for l in range(step // 128):
            bounce[l] = pw[:, c + l * 128 : c + (l + 1) * 128].astype(F32)
        mixed = jnp.concatenate([
            jnp.concatenate([bounce[l, pl.ds(k, lats, groups), :] for k in range(groups)], axis=0)
            for l in range(step // 128)
        ], axis=1)
        pwf[:, c : c + step] = mixed
        total_w = total_w + lanes_sum(mixed)
        total_b = total_b + lanes_sum(pb[pl.ds(c, step)].reshape(1, step))
    mean = jnp.sum(total_w, axis=1, keepdims=True) / width
    mean_b = jnp.sum(total_b, axis=1, keepdims=True) / width
    at16 = lax.broadcasted_iota(jnp.int32, (16, step), 0)
    for c in range(0, width, step):
        gains = 1.0 + scale[pl.ds(c, step)].reshape(1, step)
        center = pwf[:, c : c + step] - mean
        center_b = pb[pl.ds(c, step)].reshape(1, step) - mean_b
        moved = shift[pl.ds(c, step)].reshape(1, step)
        last = jnp.where(at16 == 0, center_b * gains, jnp.where(at16 == 1, moved, 0.0))
        for k, piece in enumerate(split(center * gains)):
            mod[pl.ds(k * rows_m, feats), c : c + step] = piece
        for k, piece in enumerate(split(last)):
            mod[pl.ds(k * rows_m + feats, 16), c : c + step] = piece
        last = jnp.where(at16 == 0, center_b, 0.0)
        for k, piece in enumerate(split(center)):
            cen[pl.ds(k * rows_m, feats), c : c + step] = piece
        for k, piece in enumerate(split(last)):
            cen[pl.ds(k * rows_m + feats, 16), c : c + step] = piece

    def gram_of(v):
        g = lax.dot_general(v, v, nt, preferred_element_type=F32)
        return g[0:rows_m, 0:rows_m] + g[0:rows_m, rows_m:] + g[rows_m:, 0:rows_m] + g[rows_m:, rows_m:]

    lower = lax.broadcasted_iota(jnp.int32, (feats // 2, 128), 1) < feats

    def pack(v, ref):
        gram[:, 0:rows_m] = gram_of(v)
        ref[pl.ds(0, feats // 2), :] = jnp.where(
            lower, gram[0 : feats // 2, :], pltpu.roll(gram[feats // 2 : feats, :], feats, 1)
        )
        ref[pl.ds(feats // 2, 8), :] = gram[feats : feats + 8, :]

    gram[...] = jnp.zeros(gram.shape, F32)
    pack(cen[...], gram_out.at[0])
    for h, (bias, gains) in enumerate(((qb, qg), (kb, kg))):
        for n in range(count_n):
            at = pl.ds(n * tile, tile)
            rows_qk[h * count_n + n, 0:1, :] = bias[at].reshape(1, tile)
            rows_qk[h * count_n + n, 1:2, :] = gains[at].reshape(1, tile)
    mat[pl.ds(2 * feats + 16, 2 * feats - 16), :] = jnp.zeros((2 * feats - 16, 2 * part), BF16)
    at_row = lax.broadcasted_iota(jnp.int32, (rows_m, tile), 0)
    at_last = lax.broadcasted_iota(jnp.int32, (16, tile), 0)

    def project(g):
        to = pl.ds(pl.multiple_of(g * tile, tile), tile)
        v = dot(mod[...], w_all[g])
        v = v[0:rows_m] + v[rows_m:] + jnp.where(at_row == feats + 1, rows_qk[g, 0:1, :], 0.0)
        for k, piece in enumerate(split(v)):
            m_all[pl.ds(k * rows_m, rows_m), to] = piece
        v = v * rows_qk[g, 1:2, :]
        for k, piece in enumerate(split(v[0:feats])):
            mat[pl.ds(k * feats, feats), to] = piece
        m, c = v[feats : feats + 1], v[feats + 1 : feats + 2]
        m_hi, c_hi = m.astype(BF16).astype(F32), c.astype(BF16).astype(F32)
        last = jnp.where(at_last % 2 == 0, c_hi, c - c_hi)
        last = jnp.where(at_last == 0, m_hi, jnp.where(at_last == 1, m - m_hi, last))
        mat[pl.ds(2 * feats, 16), to] = jnp.where(at_last < 8, last, 0.0).astype(BF16)

    def both(p, carry):
        for g in (2 * p, 2 * p + 1):
            pltpu.make_async_copy(wq_h.at[:, pl.ds(0, tile)], w_all.at[g], wsem.at[g]).wait()
        for g in (2 * p, 2 * p + 1):
            project(g)
        return carry

    def share(h):
        pack(m_all[:, pl.ds(h * part, part)], gram_s.at[h])
        out = [
            pltpu.make_async_remote_copy(
                src_ref=gram_s.at[h], dst_ref=gram_r.at[i - 1, h], send_sem=ss_sem.at[h, i - 1],
                recv_sem=sr_sem.at[h, i - 1], device_id=(lax.rem(t + i, count_t), r), device_id_type=MESH,
            )
            for i in range(1, count_t)
        ]
        for c in out:
            c.start()
        return out

    lax.fori_loop(0, 1, both, 0)
    for copy, p in zip(halo, plan):
        def take(copy=copy, p=p):
            copy.wait_recv()
            for k, i in enumerate(p[6]):
                tot[pl.ds(i * lats, lats), :] += rcv[pl.ds((p[0] + k) * lats, lats), :]
        pl.when(p[5])(take)

    lane = lax.broadcasted_iota(jnp.int32, (lats, cols), 1)
    for q in range(2):
        f0, f1 = tot[pl.ds(q * lats, lats), :], tot[pl.ds((2 + q) * lats, lats), :]
        lat_all[own, pl.ds(2 * q * lats, lats), :] = jnp.where(lane < half, f0, pltpu.roll(f1, half, 1)).astype(BF16)
        lat_all[own, pl.ds((2 * q + 1) * lats, lats), :] = jnp.where(lane < half, pltpu.roll(f0, half, 1), f1).astype(BF16)

    inner = 1
    while inner * inner * 4 <= count_r and count_r % (inner * 2) == 0:
        inner *= 2
    outer = count_r // inner
    chips = count_t // 2
    flat = chips * inner
    side, chip = lax.rem(t, 2), t // 2
    far, near = r // inner, lax.rem(r, inner)
    spot = chip * inner + near
    turn = 1 - 2 * lax.min(far // max(outer // 2, 1), 1)

    def line_at(i):
        return lax.rem(far + turn * i + outer, outer)

    def device(z, p):
        return (p // inner) * 2 + side, z * inner + lax.rem(p, inner)

    def ident_of(z, p, s):
        return ((p // inner) * 2 + s) * count_r + z * inner + lax.rem(p, inner)

    def send(ident, dt, dr, sem):
        return pltpu.make_async_remote_copy(
            src_ref=lat_all.at[ident], dst_ref=lat_all.at[ident], send_sem=as_sem.at[sem], recv_sem=ar_sem.at[ident],
            device_id=(dt, dr), device_id_type=MESH,
        )

    def to_line(i):
        dt, dr = device(line_at(i), spot)
        return send(own, dt, dr, i - 1)

    def to_plane(i, k):
        dt, dr = device(far, lax.rem(spot + k, flat))
        return send(ident_of(line_at(i), spot, side), dt, dr, outer - 1 + i * flat + k)

    def to_mate(i, k):
        ident = ident_of(line_at(i), lax.rem(spot + flat - k, flat), side)
        return send(ident, t + 1 - 2 * side, r, outer - 1 + outer * flat + i * flat + k)

    def from_mate(i, k):
        return send(ident_of(line_at(i), lax.rem(spot + k, flat), 1 - side), t, r, 0)

    for i in range(1, outer):
        to_line(i).start()
    for k in range(1, flat):
        to_plane(0, k).start()
    to_mate(0, 0).start()

    def relay_line(i):
        to_mate(i, 0).wait_recv()
        for k in range(1, flat):
            to_plane(i, k).start()
        to_mate(i, 0).start()

    def relay_plane(i):
        def one(k, c):
            copy = to_mate(i, k)
            copy.wait_recv()
            copy.start()
            return c

        lax.fori_loop(1, flat, one, 0)

    middle = -(-count_n // 2)
    lax.fori_loop(1, middle, both, 0)
    if outer > 1:
        relay_line(1)
    shares = [share(0)]
    between = (middle + count_n) // 2
    lax.fori_loop(middle, between, both, 0)
    for i in range(2, outer - 1):
        relay_line(i)
    lax.fori_loop(between, count_n, both, 0)
    shares.append(share(1))
    if outer > 2:
        relay_line(outer - 1)

    for i in range(outer):
        relay_plane(i)
    for i in range(outer):
        lax.fori_loop(0, flat, lambda k, c, i=i: (from_mate(i, k).wait_recv(), c)[1], 0)

    for h in range(2):
        gram_out[1 + h] = gram_s[h]
        for i, c in enumerate(shares[h]):
            c.wait_recv()
            gram_out[1 + h] += gram_r[i, h]

    def pick(j, carry):
        x_out[j] = lat_all[packing[r * count_t + j]]
        return carry

    lax.fori_loop(0, count_t, pick, 0)

    for copy, p in zip(halo, plan):
        pl.when(p[4])(copy.wait_send)
    for i in range(1, outer):
        to_line(i).wait_send()
    for i in range(outer):
        for k in range(1, flat):
            to_plane(i, k).wait_send()
        for k in range(flat):
            to_mate(i, k).wait_send()
    for c in shares[0] + shares[1]:
        c.wait_send()


def per_device(
    features, block_gain, conv_weight, conv_bias, latent_weight, latent_bias, patch_weight, patch_bias,
    shift_mod, scale_mod, query_weight, query_bias, query_gain, key_weight, key_bias, key_gain, packing,
):
    count_t, count_r = lax.axis_size("tm"), lax.axis_size("rows")
    count = count_t * count_r
    _, _, cols, chans = features.shape
    feats, width = patch_weight.shape
    lats = latent_weight.shape[1]
    part = query_weight.shape[1]
    tile = 256 if part % 256 == 0 else 128
    V = pltpu.VMEM
    rows_m = feats + 16
    operands = (
        packing, features, block_gain, conv_weight, conv_bias, latent_weight.T, latent_bias, patch_weight, patch_bias,
        shift_mod, scale_mod, query_weight, query_bias, query_gain, key_weight, key_bias, key_gain,
    )
    like = lambda a: V(a.shape, a.dtype)
    scratch = [pltpu.SMEM(packing.shape, packing.dtype)] + [like(a) for a in operands[1:11]]
    scratch += [
        V((2 * part // tile, width, tile), BF16),
        V((part,), F32),
        V((part,), F32),
        V((part,), F32),
        V((part,), F32),
        V((2 * part // tile, 8, tile), F32),
        V((2, chans // 128, cols, 128), F32),
        V((9 * lats, 4 * chans), BF16),
        V((4 * cols, 4 * chans), BF16),
        V((9 * lats, 4 * cols), F32),
        V((12 * lats, cols), F32),
        V((12 * lats, cols), F32),
        V((4 * lats, cols), F32),
        V((count, feats, cols), BF16),
        V((feats, width), F32),
        V((4, feats, 128), F32),
        V((2 * rows_m, width), BF16),
        V((2 * rows_m, width), BF16),
        V((2 * rows_m, 2 * part), BF16),
        V((rows_m, 128), F32),
        V((2, feats // 2 + 8, 128), F32),
        V((count_t - 1, 2, feats // 2 + 8, 128), F32),
    ]
    dma = pltpu.SemaphoreType.DMA
    scratch += [
        dma((14,)), dma((9,)), dma((2 * part // tile,)), dma((5,)), dma((5,)), dma((count + count_r,)), dma((count,)),
        dma((2, count_t - 1)), dma((2, count_t - 1)),
    ]
    outs = (
        jax.ShapeDtypeStruct((count_t, feats, cols), BF16),
        jax.ShapeDtypeStruct((4 * feats, 2 * part), BF16),
        jax.ShapeDtypeStruct((3, feats // 2 + 8, 128), F32),
    )
    x, mat, gram = pl.pallas_call(
        functools.partial(kernel, count_t, count_r),
        out_shape=outs,
        in_specs=[pl.BlockSpec(memory_space=pltpu.HBM)] * 17,
        out_specs=(pl.BlockSpec(memory_space=V),) * 3,
        scratch_shapes=scratch,
        compiler_params=pltpu.CompilerParams(collective_id=0, has_side_effects=True, vmem_limit_bytes=52 * 2**20),
    )(*[pltpu.with_memory_space_constraint(a, pltpu.HBM) for a in operands])
    return finish(width, x, mat, gram)


def final(width, x_ref, mat, gram, q_h, k_h, left, coef, tiles, osem):
    count_t, feats, cols = x_ref.shape
    part = mat.shape[1] // 2
    tokens = left.shape[0]
    tile = tiles.shape[2]
    for j in range(count_t):
        x = x_ref[j].astype(F32)
        left[pl.ds(j * cols, cols), 0:128] = jnp.concatenate([x, x], axis=0).T.astype(BF16)
    lane = lax.broadcasted_iota(jnp.int32, (1, 128), 1)
    hf = feats // 2

    def entry(h, row, at):
        return jnp.sum(jnp.where(lane == at, gram[h, hf + row : hf + row + 1, :], 0.0), axis=1, keepdims=True)

    def cross(h, row):
        return jnp.where(lane < feats, 2.0 * gram[h, hf + row : hf + row + 1, :], 0.0)

    quads = []
    for h in range(3):
        top = gram[h, 0:hf, :]
        square = jnp.where(lane < feats, jnp.concatenate([top, pltpu.roll(top, feats, 1)], axis=0), 0.0)
        quads.append(jnp.concatenate(split(square), axis=0))
    stacked = jnp.concatenate(quads, axis=1)
    rows = 128
    at_lane = lax.broadcasted_iota(jnp.int32, (rows, 128), 1)
    for c in range(0, tokens, rows):
        at = pl.ds(c, rows)
        prod = dot(left[at, 0:128], stacked)
        y = left[at, 0:128].astype(F32)
        e = jnp.sum(y * (prod[:, 0:128] + cross(0, 0)), axis=1, keepdims=True) + entry(0, 0, feats)
        var = e / width + epsilon
        inv = lax.rsqrt(var)
        sigma = jnp.broadcast_to(var * inv, (rows, 128))
        high = sigma.astype(BF16).astype(F32)
        mid = (sigma - high).astype(BF16).astype(F32)
        ends = jnp.where(at_lane < 6, mid, sigma - high - mid)
        ends = jnp.where(at_lane < 2, 1.0, jnp.where(at_lane < 4, high, ends))
        left[at, 128:256] = jnp.where(at_lane < 8, ends, 0.0).astype(BF16)
        for h in range(1, 3):
            body = inv * (prod[:, h * 128 : (h + 1) * 128] + cross(h, 0)) + cross(h, 1)
            ss = inv * jnp.sum(y * body, axis=1, keepdims=True) + inv * inv * entry(h, 0, feats)
            ss = ss + 2.0 * inv * entry(h, 0, feats + 1) + entry(h, 1, feats + 1)
            coef[h - 1, at, :] = jnp.broadcast_to(lax.rsqrt(ss / width + epsilon) * inv, (rows, 128))
    count_n = part // tile

    def out_copy(i, n, dst):
        return pltpu.make_async_copy(tiles.at[i * count_n + n], dst.at[:, pl.ds(n * tile, tile)], osem.at[i, n])

    for i, dst in enumerate((q_h, k_h)):
        for n in range(count_n):
            for c in range(0, tokens, 256):
                at = pl.ds(c, 256)
                v = dot(left[at, :], mat[:, pl.ds(i * part + n * tile, tile)])
                for l in range(0, tile, 128):
                    o = coef[i, at, :] * v[:, l : l + 128]
                    tiles[i * count_n + n, at, pl.ds(l, 128)] = o.astype(BF16)
            out_copy(i, n, dst).start()
    for i, dst in enumerate((q_h, k_h)):
        for n in range(count_n):
            out_copy(i, n, dst).wait()


def finish(width, x, mat, gram):
    count_t, feats, cols = x.shape
    tokens, part = count_t * cols, mat.shape[1] // 2
    tile = 256 if part % 256 == 0 else 128
    out = jax.ShapeDtypeStruct((tokens, part), BF16)
    V, dma = pltpu.VMEM, pltpu.SemaphoreType.DMA
    return pl.pallas_call(
        functools.partial(final, width),
        out_shape=(out, out),
        in_specs=[pl.BlockSpec(memory_space=V)] * 3,
        out_specs=(pl.BlockSpec(memory_space=pl.ANY),) * 2,
        scratch_shapes=[
            V((tokens, 4 * feats), BF16), V((2, tokens, 128), F32), V((2 * part // tile, tokens, tile), BF16),
            dma((2, part // tile)),
        ],
        compiler_params=pltpu.CompilerParams(vmem_limit_bytes=24 * 2**20),
    )(x, mat, gram)


def solution(mesh):
    in_specs = (
        P("tm", "rows", None, None), P(), P(), P(), P(), P(), P(), P(), P(), P(),
        P(None, "tm"), P("tm"), P("tm"), P(None, "tm"), P("tm"), P("tm"), P(),
    )
    out_specs = (P("rows", "tm"), P("rows", "tm"))
    return jax.shard_map(per_device, mesh=mesh, in_specs=in_specs, out_specs=out_specs, check_vma=False)
```

time: 40.9 us -> 26.5 us (0.65); the launches traced: 40.2 us -> 26.3 us
  local copies, waits for them, and re-layouts: 10.4 us -> 0 us
  Pallas kernels: 29.1 us -> 25.7 us
    unnamed x28 -> x0, local copies, waits for them, and re-layouts: 10.4 us -> none
    pallas_call x1, Pallas kernels: 26.6 us -> 23.3 us  [per_device(): pl.pallas_call(functools.partial(kernel, count_t, count_r), out_shape=out...]
where the time goes in v2:
time: 26.5 us; the launch traced here: 26.3 us
  Pallas kernels  25.7 us (97%)
  between operations  0.65 us (2%)
    pallas_call x1, Pallas kernels, per_device(): pl.pallas_call(functools.partial(kernel, count_t, count_r), out_shape=out...  23.3 us
    pallas_call x1, Pallas kernels, finish(): pl.pallas_call(functools.partial(final, width), out_shape=(out, out), in_...  2.4 us

profile of v2, /device:TPU:1, one launch (start us, length us, event | category | flops | bytes accessed | tf_op | source)
XLA Modules:
  0.0 26.3 jit_solution(1870326560567623200)
XLA Ops:
  0.6 23.3 %shard_map.176 = (bf16[4,64,128]{2,1,0:T(8,128)(2,1)S(1)}, bf16[256,2560]{1,0:T(8,128)(2,1)S(1)}, f32[3,40,128]{2,1,0:T(8,128)S(1)}) custom-call(s32[32]{0:T(128)} %packing_h.1, bf16[2,2,128,384]{3,2,1,0:T(8,128)(2,1)} %feat_h.1, f32[384]{0:T(512)} %gain_h.1, bf16[3,3,3,384,384]{4,3,2,1,0:T(8,128)(2,1)} %conv_h.1, f32[384]{0:T(512)} %cbias_h.1, ...), custom_call_target="tpu_custom_call" | custom-call | tf_op jit(solution)/shard_map/pallas_call | solution.py:430
  23.9 2.4 %shard_map.177 = (bf16[512,1280]{1,0:T(8,128)(2,1)}, bf16[512,1280]{1,0:T(8,128)(2,1)}) custom-call(bf16[4,64,128]{2,1,0:T(8,128)(2,1)S(1)} %get-tuple-element.5.x_ref, bf16[256,2560]{1,0:T(8,128)(2,1)S(1)} %get-tuple-element.6.mat, f32[3,40,128]{2,1,0:T(8,128)S(1)} %get-tuple-element.7.gram), custom_call_target="tpu_custom_call" | custom-call | tf_op jit(solution)/shard_map/pallas_call | solution.py:509

commit v3 on v2

--- a/solution.py
+++ b/solution.py
@@ -209,7 +209,6 @@
         ref[pl.ds(feats // 2, 8), :] = gram[feats : feats + 8, :]
 
     gram[...] = jnp.zeros(gram.shape, F32)
-    pack(cen[...], gram_out.at[0])
     for h, (bias, gains) in enumerate(((qb, qg), (kb, kg))):
         for n in range(count_n):
             at = pl.ds(n * tile, tile)
@@ -254,7 +253,9 @@
             c.start()
         return out
 
-    lax.fori_loop(0, 1, both, 0)
+    middle = -(-count_n // 2)
+    ahead = min(2, middle)
+    lax.fori_loop(0, ahead, both, 0)
     for copy, p in zip(halo, plan):
         def take(copy=copy, p=p):
             copy.wait_recv()
@@ -277,10 +278,14 @@
     side, chip = lax.rem(t, 2), t // 2
     far, near = r // inner, lax.rem(r, inner)
     spot = chip * inner + near
-    turn = 1 - 2 * lax.min(far // max(outer // 2, 1), 1)
+    flip = lax.min(far // max(outer // 2, 1), 1)
+    mirror = far + flip * (outer - 1 - 2 * far)
 
     def line_at(i):
-        return lax.rem(far + turn * i + outer, outer)
+        v = lax.rem(mirror + i, outer)
+        if outer == 4:
+            v = (mirror, mirror + 1, 2 - 2 * mirror, mirror * 0 + 3)[i]
+        return v + flip * (outer - 1 - 2 * v)
 
     def device(z, p):
         return (p // inner) * 2 + side, z * inner + lax.rem(p, inner)
@@ -309,16 +314,32 @@
     def from_mate(i, k):
         return send(ident_of(line_at(i), lax.rem(spot + k, flat), 1 - side), t, r, 0)
 
+    def to_far(k):
+        dt, dr = device(line_at(outer - 1), lax.rem(spot + k, flat))
+        return send(own, dt, dr, outer - 1 + (outer - 1) * flat + k)
+
     for i in range(1, outer):
         to_line(i).start()
     for k in range(1, flat):
         to_plane(0, k).start()
+    if outer > 1:
+        @pl.when(mirror == 0)
+        def _():
+            for k in range(1, flat):
+                to_far(k).start()
     to_mate(0, 0).start()
 
     def relay_line(i):
         to_mate(i, 0).wait_recv()
-        for k in range(1, flat):
-            to_plane(i, k).start()
+
+        def forward():
+            for k in range(1, flat):
+                to_plane(i, k).start()
+
+        if i == outer - 1:
+            pl.when(mirror > 0)(forward)
+        else:
+            forward()
         to_mate(i, 0).start()
 
     def relay_plane(i):
@@ -330,21 +351,22 @@
 
         lax.fori_loop(1, flat, one, 0)
 
-    middle = -(-count_n // 2)
-    lax.fori_loop(1, middle, both, 0)
+    lax.fori_loop(ahead, middle, both, 0)
+    shares = [share(0)]
     if outer > 1:
         relay_line(1)
-    shares = [share(0)]
     between = (middle + count_n) // 2
     lax.fori_loop(middle, between, both, 0)
-    for i in range(2, outer - 1):
-        relay_line(i)
+    if outer > 2:
+        relay_line(2)
     lax.fori_loop(between, count_n, both, 0)
     shares.append(share(1))
-    if outer > 2:
-        relay_line(outer - 1)
-
-    for i in range(outer):
+    for i in range(3, outer):
+        relay_line(i)
+    relay_plane(0)
+    pack(cen[...], gram_out.at[0])
+
+    for i in range(1, outer):
         relay_plane(i)
     for i in range(outer):
         lax.fori_loop(0, flat, lambda k, c, i=i: (from_mate(i, k).wait_recv(), c)[1], 0)
@@ -443,44 +465,42 @@
     part = mat.shape[1] // 2
     tokens = left.shape[0]
     tile = tiles.shape[2]
-    for j in range(count_t):
-        x = x_ref[j].astype(F32)
-        left[pl.ds(j * cols, cols), 0:128] = jnp.concatenate([x, x], axis=0).T.astype(BF16)
     lane = lax.broadcasted_iota(jnp.int32, (1, 128), 1)
     hf = feats // 2
+    quads, ends = [], []
+    for h in range(3):
+        top, tail = gram[h, 0:hf, :], gram[h, hf : hf + 8, :]
+        square = jnp.where(lane < feats, jnp.concatenate([top, pltpu.roll(top, feats, 1)], axis=0), 0.0)
+        quads.append(square)
+        ends.append(jnp.where(lane < feats, tail, 0.0))
 
     def entry(h, row, at):
         return jnp.sum(jnp.where(lane == at, gram[h, hf + row : hf + row + 1, :], 0.0), axis=1, keepdims=True)
 
-    def cross(h, row):
-        return jnp.where(lane < feats, 2.0 * gram[h, hf + row : hf + row + 1, :], 0.0)
-
-    quads = []
-    for h in range(3):
-        top = gram[h, 0:hf, :]
-        square = jnp.where(lane < feats, jnp.concatenate([top, pltpu.roll(top, feats, 1)], axis=0), 0.0)
-        quads.append(jnp.concatenate(split(square), axis=0))
-    stacked = jnp.concatenate(quads, axis=1)
-    rows = 128
-    at_lane = lax.broadcasted_iota(jnp.int32, (rows, 128), 1)
-    for c in range(0, tokens, rows):
-        at = pl.ds(c, rows)
-        prod = dot(left[at, 0:128], stacked)
-        y = left[at, 0:128].astype(F32)
-        e = jnp.sum(y * (prod[:, 0:128] + cross(0, 0)), axis=1, keepdims=True) + entry(0, 0, feats)
-        var = e / width + epsilon
+    hi, lo = split(jnp.concatenate(quads + ends, axis=0))
+    lo_at = pltpu.roll(lo.astype(F32), feats, 1).astype(BF16)
+    stacked = hi + lo_at
+    at16 = lax.broadcasted_iota(jnp.int32, (16, cols), 0)
+    for j in range(count_t):
+        x = x_ref[j]
+        prod = dot(stacked, jnp.concatenate([x, x], axis=0))
+        x = x.astype(F32)
+        line = lambda h, row: prod[3 * feats + 8 * h + row : 3 * feats + 8 * h + row + 1, :]
+        square = lambda h: jnp.sum(x * prod[h * feats : (h + 1) * feats, :], axis=0, keepdims=True)
+        var = (square(0) + 2.0 * line(0, 0) + entry(0, 0, feats)) / width + epsilon
         inv = lax.rsqrt(var)
-        sigma = jnp.broadcast_to(var * inv, (rows, 128))
+        sigma = var * inv
         high = sigma.astype(BF16).astype(F32)
         mid = (sigma - high).astype(BF16).astype(F32)
-        ends = jnp.where(at_lane < 6, mid, sigma - high - mid)
-        ends = jnp.where(at_lane < 2, 1.0, jnp.where(at_lane < 4, high, ends))
-        left[at, 128:256] = jnp.where(at_lane < 8, ends, 0.0).astype(BF16)
+        more = jnp.where(at16 < 4, high, jnp.where(at16 < 6, mid, sigma - high - mid))
+        more = jnp.where(at16 < 2, 1.0, jnp.where(at16 < 8, more, 0.0))
+        at = pl.ds(j * cols, cols)
+        rest = jnp.zeros((2 * feats - 16, cols), F32)
+        left[at, :] = jnp.concatenate([x, x, more, rest], axis=0).T.astype(BF16)
         for h in range(1, 3):
-            body = inv * (prod[:, h * 128 : (h + 1) * 128] + cross(h, 0)) + cross(h, 1)
-            ss = inv * jnp.sum(y * body, axis=1, keepdims=True) + inv * inv * entry(h, 0, feats)
-            ss = ss + 2.0 * inv * entry(h, 0, feats + 1) + entry(h, 1, feats + 1)
-            coef[h - 1, at, :] = jnp.broadcast_to(lax.rsqrt(ss / width + epsilon) * inv, (rows, 128))
+            ss = inv * inv * (square(h) + 2.0 * line(h, 0) + entry(h, 0, feats))
+            ss = ss + 2.0 * inv * (line(h, 1) + entry(h, 0, feats + 1)) + entry(h, 1, feats + 1)
+            coef[h - 1, at, :] = jnp.broadcast_to(lax.rsqrt(ss / width + epsilon) * inv, (128, cols)).T
     count_n = part // tile
 
     def out_copy(i, n, dst):

time: 26.5 us -> 25.2 us (0.951)
  the two profiles are of different devices: /device:TPU:1 before, /device:TPU:17 now
where the time goes in v3:
time: 25.2 us; the launch traced here: 25.1 us
  Pallas kernels  24.4 us (97%)
  between operations  0.65 us (3%)
    pallas_call x1, Pallas kernels, per_device(): pl.pallas_call(functools.partial(kernel, count_t, count_r), out_shape=out...  22.1 us
    pallas_call x1, Pallas kernels, finish(): pl.pallas_call(functools.partial(final, width), out_shape=(out, out), in_...  2.34 us

profile of v3, /device:TPU:17, one launch (start us, length us, event | category | flops | bytes accessed | tf_op | source)
XLA Modules:
  0.0 25.1 jit_solution(7898261908009083248)
XLA Ops:
  0.6 22.1 %shard_map.176 = (bf16[4,64,128]{2,1,0:T(8,128)(2,1)S(1)}, bf16[256,2560]{1,0:T(8,128)(2,1)S(1)}, f32[3,40,128]{2,1,0:T(8,128)S(1)}) custom-call(s32[32]{0:T(128)} %packing_h.1, bf16[2,2,128,384]{3,2,1,0:T(8,128)(2,1)} %feat_h.1, f32[384]{0:T(512)} %gain_h.1, bf16[3,3,3,384,384]{4,3,2,1,0:T(8,128)(2,1)} %conv_h.1, f32[384]{0:T(512)} %cbias_h.1, ...), custom_call_target="tpu_custom_call" | custom-call | tf_op jit(solution)/shard_map/pallas_call | solution.py:452
  22.7 2.3 %shard_map.177 = (bf16[512,1280]{1,0:T(8,128)(2,1)}, bf16[512,1280]{1,0:T(8,128)(2,1)}) custom-call(bf16[4,64,128]{2,1,0:T(8,128)(2,1)S(1)} %get-tuple-element.5.x_ref, bf16[256,2560]{1,0:T(8,128)(2,1)S(1)} %get-tuple-element.6.mat, f32[3,40,128]{2,1,0:T(8,128)S(1)} %get-tuple-element.7.gram), custom_call_target="tpu_custom_call" | custom-call | tf_op jit(solution)/shard_map/pallas_call | solution.py:529

commit v4 on v3

--- a/solution.py
+++ b/solution.py
@@ -49,11 +49,14 @@
     ]
     copies = [pltpu.make_async_copy(s, d, lsem.at[i]) for i, (s, d) in enumerate(early + late)]
     first, later = copies[: len(early)], copies[len(early) :]
-    taps = [pltpu.make_async_copy(conv_h.at[i // 3, i % 3], conv.at[i // 3, i % 3], csem.at[i]) for i in range(9)]
+    runs = [(0, 2), (2, 2), (4, 2), (6, 2), (8, 1)]
+    taps = [
+        pltpu.make_async_copy(conv_h.at[pl.ds(i, n)], conv.at[pl.ds(i, n)], csem.at[k]) for k, (i, n) in enumerate(runs)
+    ]
     for c in first + taps + later:
         c.start()
     loads = [
-        pltpu.make_async_copy(w.at[:, pl.ds(n * tile, tile)], w_all.at[h * count_n + n], wsem.at[h * count_n + n])
+        pltpu.make_async_copy(w.at[:, pl.ds(n * tile, tile)], w_all.at[h * count_n + n], wsem.at[(h * count_n + n) // 2])
         for h, w in enumerate((wq_h, wk_h)) for n in range(count_n)
     ]
 
@@ -97,16 +100,15 @@
     km[:, pl.ds(3 * chans, chans)] = jnp.zeros((9 * lats, chans), BF16)
     km[pl.ds(7 * lats, lats), pl.ds(3 * chans, chans)] = lwv
     started = 0
-    for p in range(5):
-        ids = [i for i in (2 * p, 2 * p + 1) if i < 9]
-        for i in ids:
-            taps[i].wait()
+    for p, (i, n) in enumerate(runs):
+        ids = range(i, i + n)
+        taps[p].wait()
         more = min(len(loads), (p + 1) * -(-len(loads) // 5))
         for c in loads[started:more]:
             c.start()
         started = more
         for e in range(3):
-            rhs = jnp.concatenate([conv[i // 3, i % 3, e] for i in ids], axis=1)
+            rhs = jnp.concatenate([conv[i, e] for i in ids], axis=1)
             left = pair if len(ids) == 2 else lwv
             folded = lax.dot_general(left, rhs, nt, preferred_element_type=F32)
             km[pl.ds(ids[0] * lats, lats * len(ids)), pl.ds(e * chans, chans)] = folded.astype(BF16)
@@ -189,11 +191,6 @@
             mod[pl.ds(k * rows_m, feats), c : c + step] = piece
         for k, piece in enumerate(split(last)):
             mod[pl.ds(k * rows_m + feats, 16), c : c + step] = piece
-        last = jnp.where(at16 == 0, center_b, 0.0)
-        for k, piece in enumerate(split(center)):
-            cen[pl.ds(k * rows_m, feats), c : c + step] = piece
-        for k, piece in enumerate(split(last)):
-            cen[pl.ds(k * rows_m + feats, 16), c : c + step] = piece
 
     def gram_of(v):
         g = lax.dot_general(v, v, nt, preferred_element_type=F32)
@@ -234,8 +231,8 @@
         mat[pl.ds(2 * feats, 16), to] = jnp.where(at_last < 8, last, 0.0).astype(BF16)
 
     def both(p, carry):
-        for g in (2 * p, 2 * p + 1):
-            pltpu.make_async_copy(wq_h.at[:, pl.ds(0, tile)], w_all.at[g], wsem.at[g]).wait()
+        pair_at = w_all.at[pl.ds(2 * p, 2)]
+        pltpu.make_async_copy(pair_at, pair_at, wsem.at[p]).wait()
         for g in (2 * p, 2 * p + 1):
             project(g)
         return carry
@@ -244,17 +241,20 @@
         pack(m_all[:, pl.ds(h * part, part)], gram_s.at[h])
         out = [
             pltpu.make_async_remote_copy(
-                src_ref=gram_s.at[h], dst_ref=gram_r.at[i - 1, h], send_sem=ss_sem.at[h, i - 1],
-                recv_sem=sr_sem.at[h, i - 1], device_id=(lax.rem(t + i, count_t), r), device_id_type=MESH,
+                src_ref=gram_s.at[h], dst_ref=gram_r.at[h, i - 1], send_sem=ss_sem.at[h],
+                recv_sem=sr_sem.at[h], device_id=(lax.rem(t + i, count_t), r), device_id_type=MESH,
             )
             for i in range(1, count_t)
         ]
         for c in out:
             c.start()
-        return out
+        return pltpu.make_async_remote_copy(
+            src_ref=gram_r.at[h], dst_ref=gram_r.at[h], send_sem=ss_sem.at[h], recv_sem=sr_sem.at[h],
+            device_id=(t, r), device_id_type=MESH,
+        )
 
     middle = -(-count_n // 2)
-    ahead = min(2, middle)
+    ahead = min(1, middle)
     lax.fori_loop(0, ahead, both, 0)
     for copy, p in zip(halo, plan):
         def take(copy=copy, p=p):
@@ -273,109 +273,75 @@
     while inner * inner * 4 <= count_r and count_r % (inner * 2) == 0:
         inner *= 2
     outer = count_r // inner
-    chips = count_t // 2
-    flat = chips * inner
-    side, chip = lax.rem(t, 2), t // 2
-    far, near = r // inner, lax.rem(r, inner)
-    spot = chip * inner + near
+    flat = count_t // 2 * inner
+    group, away = outer * flat, (outer - 1) * flat
+    side = lax.rem(t, 2)
+    mate = t + 1 - 2 * side
+    far, spot = r // inner, t // 2 * inner + lax.rem(r, inner)
     flip = lax.min(far // max(outer // 2, 1), 1)
     mirror = far + flip * (outer - 1 - 2 * far)
 
-    def line_at(i):
-        v = lax.rem(mirror + i, outer)
-        if outer == 4:
-            v = (mirror, mirror + 1, 2 - 2 * mirror, mirror * 0 + 3)[i]
-        return v + flip * (outer - 1 - 2 * v)
-
-    def device(z, p):
-        return (p // inner) * 2 + side, z * inner + lax.rem(p, inner)
-
-    def ident_of(z, p, s):
-        return ((p // inner) * 2 + s) * count_r + z * inner + lax.rem(p, inner)
-
-    def send(ident, dt, dr, sem):
+    def place(i):
+        v = outer - 1 - i // flat
+        v = v - lax.max(0, lax.min(1, mirror - v + 1))
+        v = v + lax.max(0, i // flat - outer + 2) * (mirror - v)
+        p = lax.rem(spot + lax.rem(i, flat), flat)
+        return p // inner * 2, (v + flip * (outer - 1 - 2 * v)) * inner + lax.rem(p, inner)
+
+    def ident_of(i, s):
+        pt, pr = place(i)
+        return (pt + s) * count_r + pr
+
+    def send(at, dt, dr, sent, got):
         return pltpu.make_async_remote_copy(
-            src_ref=lat_all.at[ident], dst_ref=lat_all.at[ident], send_sem=as_sem.at[sem], recv_sem=ar_sem.at[ident],
+            src_ref=lat_all.at[at], dst_ref=lat_all.at[at], send_sem=as_sem.at[sent], recv_sem=ar_sem.at[got],
             device_id=(dt, dr), device_id_type=MESH,
         )
 
-    def to_line(i):
-        dt, dr = device(line_at(i), spot)
-        return send(own, dt, dr, i - 1)
-
-    def to_plane(i, k):
-        dt, dr = device(far, lax.rem(spot + k, flat))
-        return send(ident_of(line_at(i), spot, side), dt, dr, outer - 1 + i * flat + k)
-
-    def to_mate(i, k):
-        ident = ident_of(line_at(i), lax.rem(spot + flat - k, flat), side)
-        return send(ident, t + 1 - 2 * side, r, outer - 1 + outer * flat + i * flat + k)
-
-    def from_mate(i, k):
-        return send(ident_of(line_at(i), lax.rem(spot + k, flat), 1 - side), t, r, 0)
-
-    def to_far(k):
-        dt, dr = device(line_at(outer - 1), lax.rem(spot + k, flat))
-        return send(own, dt, dr, outer - 1 + (outer - 1) * flat + k)
-
-    for i in range(1, outer):
-        to_line(i).start()
-    for k in range(1, flat):
-        to_plane(0, k).start()
-    if outer > 1:
-        @pl.when(mirror == 0)
-        def _():
-            for k in range(1, flat):
-                to_far(k).start()
-    to_mate(0, 0).start()
-
-    def relay_line(i):
-        to_mate(i, 0).wait_recv()
-
-        def forward():
-            for k in range(1, flat):
-                to_plane(i, k).start()
-
-        if i == outer - 1:
-            pl.when(mirror > 0)(forward)
-        else:
-            forward()
-        to_mate(i, 0).start()
-
-    def relay_plane(i):
-        def one(k, c):
-            copy = to_mate(i, k)
-            copy.wait_recv()
-            copy.start()
-            return c
-
-        lax.fori_loop(1, flat, one, 0)
+    def spread(i):
+        pt, pr = place(i)
+        return send(own, pt + side, pr, 0, far)
+
+    def to_mate(i):
+        return send(ident_of(i, side), mate, r, 1, outer)
+
+    def all_of(n, sent, got):
+        return send(pl.ds(0, n), mate, r, sent, got)
+
+    def loop(first, last, body):
+        lax.fori_loop(first, last, lambda i, c: (body(i), c)[1], 0)
+
+    to_mate(away).start()
+    loop(0, away, lambda i: spread(i).start())
+    loop(away + 1, group, lambda i: spread(i).start())
+
+    def relay(j, first):
+        _, pr = place(j * flat)
+        all_of(flat - first, 0, pr // inner).wait_recv()
+        loop(j * flat + first, (j + 1) * flat, lambda i: to_mate(i).start())
 
     lax.fori_loop(ahead, middle, both, 0)
     shares = [share(0)]
-    if outer > 1:
-        relay_line(1)
-    between = (middle + count_n) // 2
-    lax.fori_loop(middle, between, both, 0)
-    if outer > 2:
-        relay_line(2)
-    lax.fori_loop(between, count_n, both, 0)
+    lax.fori_loop(middle, count_n, both, 0)
     shares.append(share(1))
-    for i in range(3, outer):
-        relay_line(i)
-    relay_plane(0)
+    for c in range(0, width, step):
+        center_b = jnp.where(at16 == 0, pb[pl.ds(c, step)].reshape(1, step) - mean_b, 0.0)
+        for k, piece in enumerate(split(pwf[:, c : c + step] - mean)):
+            cen[pl.ds(k * rows_m, feats), c : c + step] = piece
+        for k, piece in enumerate(split(center_b)):
+            cen[pl.ds(k * rows_m + feats, 16), c : c + step] = piece
     pack(cen[...], gram_out.at[0])
 
-    for i in range(1, outer):
-        relay_plane(i)
-    for i in range(outer):
-        lax.fori_loop(0, flat, lambda k, c, i=i: (from_mate(i, k).wait_recv(), c)[1], 0)
+    relay(outer - 1, 1)
+    for j in range(outer - 2, -1, -1):
+        relay(j, 0)
+    all_of(group, 1, outer).wait_recv()
 
     for h in range(2):
         gram_out[1 + h] = gram_s[h]
-        for i, c in enumerate(shares[h]):
-            c.wait_recv()
-            gram_out[1 + h] += gram_r[i, h]
+        shares[h].wait_recv()
+        for i in range(count_t - 1):
+            gram_out[1 + h] += gram_r[h, i]
 
     def pick(j, carry):
         x_out[j] = lat_all[packing[r * count_t + j]]
@@ -385,14 +351,9 @@
 
     for copy, p in zip(halo, plan):
         pl.when(p[4])(copy.wait_send)
-    for i in range(1, outer):
-        to_line(i).wait_send()
-    for i in range(outer):
-        for k in range(1, flat):
-            to_plane(i, k).wait_send()
-        for k in range(flat):
-            to_mate(i, k).wait_send()
-    for c in shares[0] + shares[1]:
+    all_of(group - 1, 0, outer).wait_send()
+    all_of(group, 1, outer).wait_send()
+    for c in shares:
         c.wait_send()
 
 
@@ -410,7 +371,7 @@
     V = pltpu.VMEM
     rows_m = feats + 16
     operands = (
-        packing, features, block_gain, conv_weight, conv_bias, latent_weight.T, latent_bias, patch_weight, patch_bias,
+        packing, features, block_gain, conv_weight.reshape(9, 3, chans, chans), conv_bias, latent_weight.T, latent_bias, patch_weight, patch_bias,
         shift_mod, scale_mod, query_weight, query_bias, query_gain, key_weight, key_bias, key_gain,
     )
     like = lambda a: V(a.shape, a.dtype)
@@ -437,12 +398,11 @@
         V((2 * rows_m, 2 * part), BF16),
         V((rows_m, 128), F32),
         V((2, feats // 2 + 8, 128), F32),
-        V((count_t - 1, 2, feats // 2 + 8, 128), F32),
+        V((2, count_t - 1, feats // 2 + 8, 128), F32),
     ]
     dma = pltpu.SemaphoreType.DMA
     scratch += [
-        dma((14,)), dma((9,)), dma((2 * part // tile,)), dma((5,)), dma((5,)), dma((count + count_r,)), dma((count,)),
-        dma((2, count_t - 1)), dma((2, count_t - 1)),
+        dma((14,)), dma((5,)), dma((part // tile,)), dma((5,)), dma((5,)), dma((2,)), dma((count_r + 1,)), dma((2,)), dma((2,)),
     ]
     outs = (
         jax.ShapeDtypeStruct((count_t, feats, cols), BF16),

time: 25.2 us -> 23.9 us (0.948)
  the two profiles are of different devices: /device:TPU:17 before, /device:TPU:1 now
where the time goes in v4:
time: 23.9 us; the launch traced here: 23.7 us
  Pallas kernels  23.1 us (97%)
  between operations  0.65 us (3%)
    pallas_call x1, Pallas kernels, per_device(): pl.pallas_call(functools.partial(kernel, count_t, count_r), out_shape=out...  20.7 us
    pallas_call x1, Pallas kernels, finish(): pl.pallas_call(functools.partial(final, width), out_shape=(out, out), in_...  2.34 us

profile of v4, /device:TPU:1, one launch (start us, length us, event | category | flops | bytes accessed | tf_op | source)
XLA Modules:
  0.0 23.7 jit_solution(5143696792532602563)
XLA Ops:
  0.6 20.7 %shard_map.176 = (bf16[4,64,128]{2,1,0:T(8,128)(2,1)S(1)}, bf16[256,2560]{1,0:T(8,128)(2,1)S(1)}, f32[3,40,128]{2,1,0:T(8,128)S(1)}) custom-call(s32[32]{0:T(128)} %packing_h.1, bf16[2,2,128,384]{3,2,1,0:T(8,128)(2,1)} %feat_h.1, f32[384]{0:T(512)} %gain_h.1, bf16[9,3,384,384]{3,2,1,0:T(8,128)(2,1)} %bitcast.2, f32[384]{0:T(512)} %cbias_h.1, ...), custom_call_target="tpu_custom_call" | custom-call | tf_op jit(solution)/shard_map/pallas_call | solution.py:412
  21.4 2.3 %shard_map.177 = (bf16[512,1280]{1,0:T(8,128)(2,1)}, bf16[512,1280]{1,0:T(8,128)(2,1)}) custom-call(bf16[4,64,128]{2,1,0:T(8,128)(2,1)S(1)} %get-tuple-element.5.x_ref, bf16[256,2560]{1,0:T(8,128)(2,1)S(1)} %get-tuple-element.6.mat, f32[3,40,128]{2,1,0:T(8,128)S(1)} %get-tuple-element.7.gram), custom_call_target="tpu_custom_call" | custom-call | tf_op jit(solution)/shard_map/pallas_call | solution.py:489

commit v5 on v4

--- a/solution.py
+++ b/solution.py
@@ -25,9 +25,9 @@
     count_t, count_r,
     packing_h, feat_h, gain_h, conv_h, cbias_h, lw_h, lbias_h, pw_h, pb_h, shift_h, scale_h,
     wq_h, qb_h, qg_h, wk_h, kb_h, kg_h,
-    x_out, mat, gram_out,
+    left, coef, mat,
     packing, feat, gain, conv, cbias, lw, lbias, pw, pb, shift, scale, w_all, qb, kb, qg, kg, rows_qk,
-    scr, km, lhs, y_ref, snd, rcv, tot, lat_all, pwf, bounce, mod, cen, m_all, gram, gram_s, gram_r,
+    scr, km, lhs, y_ref, snd, rcv, tot, lat_all, pwf, bounce, mod, cen, m_all, gram, gram_out, gram_s, gram_r,
     lsem, csem, wsem, hs_sem, hr_sem, as_sem, ar_sem, ss_sem, sr_sem,
 ):
     t, r = lax.axis_index("tm"), lax.axis_index("rows")
@@ -109,8 +109,7 @@
         started = more
         for e in range(3):
             rhs = jnp.concatenate([conv[i, e] for i in ids], axis=1)
-            left = pair if len(ids) == 2 else lwv
-            folded = lax.dot_general(left, rhs, nt, preferred_element_type=F32)
+            folded = lax.dot_general(pair if n == 2 else lwv, rhs, nt, preferred_element_type=F32)
             km[pl.ds(ids[0] * lats, lats * len(ids)), pl.ds(e * chans, chans)] = folded.astype(BF16)
     y_ref[...] = lax.dot_general(km[...], lhs[...], nt, preferred_element_type=F32)
 
@@ -254,7 +253,7 @@
         )
 
     middle = -(-count_n // 2)
-    ahead = min(1, middle)
+    ahead = min(2, middle)
     lax.fori_loop(0, ahead, both, 0)
     for copy, p in zip(halo, plan):
         def take(copy=copy, p=p):
@@ -277,7 +276,7 @@
     group, away = outer * flat, (outer - 1) * flat
     side = lax.rem(t, 2)
     mate = t + 1 - 2 * side
-    far, spot = r // inner, t // 2 * inner + lax.rem(r, inner)
+    far, near, chip, chips = r // inner, lax.rem(r, inner), t // 2, count_t // 2
     flip = lax.min(far // max(outer // 2, 1), 1)
     mirror = far + flip * (outer - 1 - 2 * far)
 
@@ -285,8 +284,9 @@
         v = outer - 1 - i // flat
         v = v - lax.max(0, lax.min(1, mirror - v + 1))
         v = v + lax.max(0, i // flat - outer + 2) * (mirror - v)
-        p = lax.rem(spot + lax.rem(i, flat), flat)
-        return p // inner * 2, (v + flip * (outer - 1 - 2 * v)) * inner + lax.rem(p, inner)
+        k = flat - 1 - lax.rem(i, flat)
+        other = lax.rem(chip + k // inner, chips)
+        return other * 2, (v + flip * (outer - 1 - 2 * v)) * inner + lax.rem(near + lax.rem(k, inner), inner)
 
     def ident_of(i, s):
         pt, pr = place(i)
@@ -311,14 +311,14 @@
     def loop(first, last, body):
         lax.fori_loop(first, last, lambda i, c: (body(i), c)[1], 0)
 
-    to_mate(away).start()
+    to_mate(group - 1).start()
     loop(0, away, lambda i: spread(i).start())
-    loop(away + 1, group, lambda i: spread(i).start())
-
-    def relay(j, first):
+    loop(away, group - 1, lambda i: spread(i).start())
+
+    def relay(j, skip):
         _, pr = place(j * flat)
-        all_of(flat - first, 0, pr // inner).wait_recv()
-        loop(j * flat + first, (j + 1) * flat, lambda i: to_mate(i).start())
+        all_of(flat - skip, 0, pr // inner).wait_recv()
+        loop(j * flat, (j + 1) * flat - skip, lambda i: to_mate(i).start())
 
     lax.fori_loop(ahead, middle, both, 0)
     shares = [share(0)]
@@ -343,11 +343,42 @@
         for i in range(count_t - 1):
             gram_out[1 + h] += gram_r[h, i]
 
-    def pick(j, carry):
-        x_out[j] = lat_all[packing[r * count_t + j]]
-        return carry
-
-    lax.fori_loop(0, count_t, pick, 0)
+    lane1 = lax.broadcasted_iota(jnp.int32, (1, 128), 1)
+    hf = feats // 2
+    quads, ends = [], []
+    for h in range(3):
+        top, tail = gram_out[h, 0:hf, :], gram_out[h, hf : hf + 8, :]
+        square = jnp.where(lane1 < feats, jnp.concatenate([top, pltpu.roll(top, feats, 1)], axis=0), 0.0)
+        quads.append(square)
+        ends.append(jnp.where(lane1 < feats, tail, 0.0))
+
+    def entry(h, row, at):
+        return jnp.sum(jnp.where(lane1 == at, gram_out[h, hf + row : hf + row + 1, :], 0.0), axis=1, keepdims=True)
+
+    hi, lo = split(jnp.concatenate(quads + ends, axis=0))
+    lo_at = pltpu.roll(lo.astype(F32), feats, 1).astype(BF16)
+    stacked = hi + lo_at
+    at16 = lax.broadcasted_iota(jnp.int32, (16, cols), 0)
+    for j in range(count_t):
+        x = lat_all[packing[r * count_t + j]]
+        prod = dot(stacked, jnp.concatenate([x, x], axis=0))
+        x = x.astype(F32)
+        line = lambda h, row: prod[3 * feats + 8 * h + row : 3 * feats + 8 * h + row + 1, :]
+        square = lambda h: jnp.sum(x * prod[h * feats : (h + 1) * feats, :], axis=0, keepdims=True)
+        var = (square(0) + 2.0 * line(0, 0) + entry(0, 0, feats)) / width + epsilon
+        inv = lax.rsqrt(var)
+        sigma = var * inv
+        high = sigma.astype(BF16).astype(F32)
+        mid = (sigma - high).astype(BF16).astype(F32)
+        more = jnp.where(at16 < 4, high, jnp.where(at16 < 6, mid, sigma - high - mid))
+        more = jnp.where(at16 < 2, 1.0, jnp.where(at16 < 8, more, 0.0))
+        at = pl.ds(j * cols, cols)
+        rest = jnp.zeros((2 * feats - 16, cols), F32)
+        left[at, :] = jnp.concatenate([x, x, more, rest], axis=0).T.astype(BF16)
+        for h in range(1, 3):
+            ss = inv * inv * (square(h) + 2.0 * line(h, 0) + entry(h, 0, feats))
+            ss = ss + 2.0 * inv * (line(h, 1) + entry(h, 0, feats + 1)) + entry(h, 1, feats + 1)
+            coef[h - 1, at, :] = jnp.broadcast_to(lax.rsqrt(ss / width + epsilon) * inv, (128, cols)).T
 
     for copy, p in zip(halo, plan):
         pl.when(p[4])(copy.wait_send)
@@ -397,6 +428,7 @@
         V((2 * rows_m, width), BF16),
         V((2 * rows_m, 2 * part), BF16),
         V((rows_m, 128), F32),
+        V((3, feats // 2 + 8, 128), F32),
         V((2, feats // 2 + 8, 128), F32),
         V((2, count_t - 1, feats // 2 + 8, 128), F32),
     ]
@@ -405,66 +437,29 @@
         dma((14,)), dma((5,)), dma((part // tile,)), dma((5,)), dma((5,)), dma((2,)), dma((count_r + 1,)), dma((2,)), dma((2,)),
     ]
     outs = (
-        jax.ShapeDtypeStruct((count_t, feats, cols), BF16),
+        jax.ShapeDtypeStruct((count_t * cols, 4 * feats), BF16),
+        jax.ShapeDtypeStruct((2, count_t * cols, 128), F32),
         jax.ShapeDtypeStruct((4 * feats, 2 * part), BF16),
-        jax.ShapeDtypeStruct((3, feats // 2 + 8, 128), F32),
     )
-    x, mat, gram = pl.pallas_call(
+    left, coef, mat = pl.pallas_call(
         functools.partial(kernel, count_t, count_r),
         out_shape=outs,
         in_specs=[pl.BlockSpec(memory_space=pltpu.HBM)] * 17,
         out_specs=(pl.BlockSpec(memory_space=V),) * 3,
         scratch_shapes=scratch,
-        compiler_params=pltpu.CompilerParams(collective_id=0, has_side_effects=True, vmem_limit_bytes=52 * 2**20),
+        compiler_params=pltpu.CompilerParams(collective_id=0, has_side_effects=True, vmem_limit_bytes=47 * 2**20),
     )(*[pltpu.with_memory_space_constraint(a, pltpu.HBM) for a in operands])
-    return finish(width, x, mat, gram)
-
-
-def final(width, x_ref, mat, gram, q_h, k_h, left, coef, tiles, osem):
-    count_t, feats, cols = x_ref.shape
+    return finish(left, coef, mat)
+
+
+def final(left, coef, mat, q_h, k_h, tiles, osem):
     part = mat.shape[1] // 2
     tokens = left.shape[0]
     tile = tiles.shape[2]
-    lane = lax.broadcasted_iota(jnp.int32, (1, 128), 1)
-    hf = feats // 2
-    quads, ends = [], []
-    for h in range(3):
-        top, tail = gram[h, 0:hf, :], gram[h, hf : hf + 8, :]
-        square = jnp.where(lane < feats, jnp.concatenate([top, pltpu.roll(top, feats, 1)], axis=0), 0.0)
-        quads.append(square)
-        ends.append(jnp.where(lane < feats, tail, 0.0))
-
-    def entry(h, row, at):
-        return jnp.sum(jnp.where(lane == at, gram[h, hf + row : hf + row + 1, :], 0.0), axis=1, keepdims=True)
-
-    hi, lo = split(jnp.concatenate(quads + ends, axis=0))
-    lo_at = pltpu.roll(lo.astype(F32), feats, 1).astype(BF16)
-    stacked = hi + lo_at
-    at16 = lax.broadcasted_iota(jnp.int32, (16, cols), 0)
-    for j in range(count_t):
-        x = x_ref[j]
-        prod = dot(stacked, jnp.concatenate([x, x], axis=0))
-        x = x.astype(F32)
-        line = lambda h, row: prod[3 * feats + 8 * h + row : 3 * feats + 8 * h + row + 1, :]
-        square = lambda h: jnp.sum(x * prod[h * feats : (h + 1) * feats, :], axis=0, keepdims=True)
-        var = (square(0) + 2.0 * line(0, 0) + entry(0, 0, feats)) / width + epsilon
-        inv = lax.rsqrt(var)
-        sigma = var * inv
-        high = sigma.astype(BF16).astype(F32)
-        mid = (sigma - high).astype(BF16).astype(F32)
-        more = jnp.where(at16 < 4, high, jnp.where(at16 < 6, mid, sigma - high - mid))
-        more = jnp.where(at16 < 2, 1.0, jnp.where(at16 < 8, more, 0.0))
-        at = pl.ds(j * cols, cols)
-        rest = jnp.zeros((2 * feats - 16, cols), F32)
-        left[at, :] = jnp.concatenate([x, x, more, rest], axis=0).T.astype(BF16)
-        for h in range(1, 3):
-            ss = inv * inv * (square(h) + 2.0 * line(h, 0) + entry(h, 0, feats))
-            ss = ss + 2.0 * inv * (line(h, 1) + entry(h, 0, feats + 1)) + entry(h, 1, feats + 1)
-            coef[h - 1, at, :] = jnp.broadcast_to(lax.rsqrt(ss / width + epsilon) * inv, (128, cols)).T
     count_n = part // tile
 
     def out_copy(i, n, dst):
-        return pltpu.make_async_copy(tiles.at[i * count_n + n], dst.at[:, pl.ds(n * tile, tile)], osem.at[i, n])
+        return pltpu.make_async_copy(tiles.at[i * count_n + n], dst.at[:, pl.ds(n * tile, tile)], osem.at[i])
 
     for i, dst in enumerate((q_h, k_h)):
         for n in range(count_n):
@@ -475,28 +470,24 @@
                     o = coef[i, at, :] * v[:, l : l + 128]
                     tiles[i * count_n + n, at, pl.ds(l, 128)] = o.astype(BF16)
             out_copy(i, n, dst).start()
-    for i, dst in enumerate((q_h, k_h)):
-        for n in range(count_n):
-            out_copy(i, n, dst).wait()
-
-
-def finish(width, x, mat, gram):
-    count_t, feats, cols = x.shape
-    tokens, part = count_t * cols, mat.shape[1] // 2
+    for i in range(2):
+        done = tiles.at[pl.ds(i * count_n, count_n)]
+        pltpu.make_async_copy(done, done, osem.at[i]).wait()
+
+
+def finish(left, coef, mat):
+    tokens, part = left.shape[0], mat.shape[1] // 2
     tile = 256 if part % 256 == 0 else 128
     out = jax.ShapeDtypeStruct((tokens, part), BF16)
     V, dma = pltpu.VMEM, pltpu.SemaphoreType.DMA
     return pl.pallas_call(
-        functools.partial(final, width),
+        final,
         out_shape=(out, out),
         in_specs=[pl.BlockSpec(memory_space=V)] * 3,
         out_specs=(pl.BlockSpec(memory_space=pl.ANY),) * 2,
-        scratch_shapes=[
-            V((tokens, 4 * feats), BF16), V((2, tokens, 128), F32), V((2 * part // tile, tokens, tile), BF16),
-            dma((2, part // tile)),
-        ],
-        compiler_params=pltpu.CompilerParams(vmem_limit_bytes=24 * 2**20),
-    )(x, mat, gram)
+        scratch_shapes=[V((2 * part // tile, tokens, tile), BF16), dma((2,))],
+        compiler_params=pltpu.CompilerParams(vmem_limit_bytes=12 * 2**20),
+    )(left, coef, mat)
 
 
 def solution(mesh):

time: 23.9 us -> 23.6 us (0.987)
    pallas_call x1, Pallas kernels: 2.34 us -> 1.73 us  [finish(): pl.pallas_call(final, out_shape=(out, out), in_specs=[pl.BlockSpec(memory...]
    pallas_call x1, Pallas kernels: 20.7 us -> 21.1 us  [per_device(): pl.pallas_call(functools.partial(kernel, count_t, count_r), out_shape=out...]
where the time goes in v5:
time: 23.6 us; the launch traced here: 23.5 us
  Pallas kernels  22.9 us (97%)
  between operations  0.65 us (3%)
    pallas_call x1, Pallas kernels, per_device(): pl.pallas_call(functools.partial(kernel, count_t, count_r), out_shape=out...  21.1 us
    pallas_call x1, Pallas kernels, finish(): pl.pallas_call(final, out_shape=(out, out), in_specs=[pl.BlockSpec(memory...  1.73 us

profile of v5, /device:TPU:1, one launch (start us, length us, event | category | flops | bytes accessed | tf_op | source)
XLA Modules:
  0.0 23.5 jit_solution(17313529856419516789)
XLA Ops:
  0.6 21.1 %shard_map.176 = (bf16[512,256]{1,0:T(8,128)(2,1)S(1)}, f32[2,512,128]{2,1,0:T(8,128)S(1)}, bf16[256,2560]{1,0:T(8,128)(2,1)S(1)}) custom-call(s32[32]{0:T(128)} %packing_h.1, bf16[2,2,128,384]{3,2,1,0:T(8,128)(2,1)} %feat_h.1, f32[384]{0:T(512)} %gain_h.1, bf16[9,3,384,384]{3,2,1,0:T(8,128)(2,1)} %bitcast.2, f32[384]{0:T(512)} %cbias_h.1, ...), custom_call_target="tpu_custom_call" | custom-call | tf_op jit(solution)/shard_map/pallas_call | solution.py:444
  21.8 1.7 %shard_map.177 = (bf16[512,1280]{1,0:T(8,128)(2,1)}, bf16[512,1280]{1,0:T(8,128)(2,1)}) custom-call(bf16[512,256]{1,0:T(8,128)(2,1)S(1)} %get-tuple-element.5.left, f32[2,512,128]{2,1,0:T(8,128)S(1)} %get-tuple-element.6.coef, bf16[256,2560]{1,0:T(8,128)(2,1)S(1)} %get-tuple-element.7.mat), custom_call_target="tpu_custom_call" | custom-call | tf_op jit(solution)/shard_map/pallas_call | solution.py:483

commit v6 on v5

--- a/solution.py
+++ b/solution.py
@@ -19,6 +19,13 @@
 def split(v):
     hi = v.astype(BF16)
     return hi, (v - hi.astype(F32)).astype(BF16)
+
+
+def planes(count_r):
+    inner = 1
+    while inner * inner * 4 <= count_r and count_r % (inner * 2) == 0:
+        inner *= 2
+    return count_r // inner if count_r // inner % 2 == 0 else 1
 
 
 def kernel(
@@ -49,7 +56,7 @@
     ]
     copies = [pltpu.make_async_copy(s, d, lsem.at[i]) for i, (s, d) in enumerate(early + late)]
     first, later = copies[: len(early)], copies[len(early) :]
-    runs = [(0, 2), (2, 2), (4, 2), (6, 2), (8, 1)]
+    runs = [(0, 1), (1, 2), (3, 2), (5, 2), (7, 2)]
     taps = [
         pltpu.make_async_copy(conv_h.at[pl.ds(i, n)], conv.at[pl.ds(i, n)], csem.at[k]) for k, (i, n) in enumerate(runs)
     ]
@@ -268,12 +275,9 @@
         lat_all[own, pl.ds(2 * q * lats, lats), :] = jnp.where(lane < half, f0, pltpu.roll(f1, half, 1)).astype(BF16)
         lat_all[own, pl.ds((2 * q + 1) * lats, lats), :] = jnp.where(lane < half, pltpu.roll(f0, half, 1), f1).astype(BF16)
 
-    inner = 1
-    while inner * inner * 4 <= count_r and count_r % (inner * 2) == 0:
-        inner *= 2
-    outer = count_r // inner
-    flat = count_t // 2 * inner
-    group, away = outer * flat, (outer - 1) * flat
+    outer = planes(count_r)
+    inner, flat = count_r // outer, count_t // 2 * (count_r // outer)
+    group, cross = outer * flat, outer // 2
     side = lax.rem(t, 2)
     mate = t + 1 - 2 * side
     far, near, chip, chips = r // inner, lax.rem(r, inner), t // 2, count_t // 2
@@ -288,39 +292,53 @@
         other = lax.rem(chip + k // inner, chips)
         return other * 2, (v + flip * (outer - 1 - 2 * v)) * inner + lax.rem(near + lax.rem(k, inner), inner)
 
-    def ident_of(i, s):
-        pt, pr = place(i)
-        return (pt + s) * count_r + pr
-
     def send(at, dt, dr, sent, got):
         return pltpu.make_async_remote_copy(
             src_ref=lat_all.at[at], dst_ref=lat_all.at[at], send_sem=as_sem.at[sent], recv_sem=ar_sem.at[got],
             device_id=(dt, dr), device_id_type=MESH,
         )
 
-    def spread(i):
-        pt, pr = place(i)
-        return send(own, pt + side, pr, 0, far)
-
-    def to_mate(i):
-        return send(ident_of(i, side), mate, r, 1, outer)
-
     def all_of(n, sent, got):
         return send(pl.ds(0, n), mate, r, sent, got)
 
     def loop(first, last, body):
         lax.fori_loop(first, last, lambda i, c: (body(i), c)[1], 0)
 
-    to_mate(group - 1).start()
-    loop(0, away, lambda i: spread(i).start())
-    loop(away, group - 1, lambda i: spread(i).start())
-
-    def relay(j, skip):
-        _, pr = place(j * flat)
-        all_of(flat - skip, 0, pr // inner).wait_recv()
-        loop(j * flat, (j + 1) * flat - skip, lambda i: to_mate(i).start())
+    spans = ((cross * flat, group - 1), (0, cross * flat))
+
+    def each(body):
+        for s in range(2):
+            if spans[s][1] > spans[s][0]:
+                pl.when(side == s)(functools.partial(body, s))
+
+    def spread(ident):
+        def one(i):
+            pt, pr = place(i)
+            send(ident, pt + side, pr, 0, far).start()
+
+        each(lambda s: loop(*spans[s], one))
+
+    def relay(s):
+        for j in range(outer - 1, -1, -1):
+            first, last = max(j * flat, spans[s][0]), min((j + 1) * flat, spans[s][1])
+            if last <= first:
+                continue
+            _, pr = place(first)
+            all_of(2 * (last - first), 0, pr // inner).wait_recv()
+
+            def one(i):
+                pt, pr = place(i)
+                for h in range(2):
+                    send((pt + h) * count_r + pr, mate, r, 1, outer + 1).start()
+
+            loop(first, last, one)
+
+    send(own, mate, r, 1, outer).start()
+    spread(own)
 
     lax.fori_loop(ahead, middle, both, 0)
+    all_of(1, 1, outer).wait_recv()
+    spread(mate * count_r + r)
     shares = [share(0)]
     lax.fori_loop(middle, count_n, both, 0)
     shares.append(share(1))
@@ -332,10 +350,11 @@
             cen[pl.ds(k * rows_m + feats, 16), c : c + step] = piece
     pack(cen[...], gram_out.at[0])
 
-    relay(outer - 1, 1)
-    for j in range(outer - 2, -1, -1):
-        relay(j, 0)
-    all_of(group, 1, outer).wait_recv()
+    each(relay)
+    counts = [2 * (last - first) for first, last in spans]
+    for s in range(2):
+        if counts[1 - s]:
+            pl.when(side == s)(lambda s=s: all_of(counts[1 - s], 1, outer + 1).wait_recv())
 
     for h in range(2):
         gram_out[1 + h] = gram_s[h]
@@ -382,8 +401,9 @@
 
     for copy, p in zip(halo, plan):
         pl.when(p[4])(copy.wait_send)
-    all_of(group - 1, 0, outer).wait_send()
-    all_of(group, 1, outer).wait_send()
+    each(lambda s: all_of(counts[s], 0, outer).wait_send())
+    for s in range(2):
+        pl.when(side == s)(lambda s=s: all_of(counts[s] + 1, 1, outer).wait_send())
     for c in shares:
         c.wait_send()
 
@@ -434,7 +454,7 @@
     ]
     dma = pltpu.SemaphoreType.DMA
     scratch += [
-        dma((14,)), dma((5,)), dma((part // tile,)), dma((5,)), dma((5,)), dma((2,)), dma((count_r + 1,)), dma((2,)), dma((2,)),
+        dma((14,)), dma((5,)), dma((part // tile,)), dma((5,)), dma((5,)), dma((2,)), dma((planes(count_r) + 2,)), dma((2,)), dma((2,)),
     ]
     outs = (
         jax.ShapeDtypeStruct((count_t * cols, 4 * feats), BF16),

time: 23.6 us -> 23.8 us (level)
  the two profiles are of different devices: /device:TPU:1 before, /device:TPU:0 now
where the time goes in v6:
time: 23.8 us; the launch traced here: 23.7 us
  Pallas kernels  23 us (97%)
  between operations  0.65 us (3%)
    pallas_call x1, Pallas kernels, per_device(): pl.pallas_call(functools.partial(kernel, count_t, count_r), out_shape=out...  21.3 us
    pallas_call x1, Pallas kernels, finish(): pl.pallas_call(final, out_shape=(out, out), in_specs=[pl.BlockSpec(memory...  1.73 us

profile of v6, /device:TPU:0, one launch (start us, length us, event | category | flops | bytes accessed | tf_op | source)
XLA Modules:
  0.0 23.7 jit_solution(10967484918398254726)
XLA Ops:
  0.6 21.3 %shard_map.176 = (bf16[512,256]{1,0:T(8,128)(2,1)S(1)}, f32[2,512,128]{2,1,0:T(8,128)S(1)}, bf16[256,2560]{1,0:T(8,128)(2,1)S(1)}) custom-call(s32[32]{0:T(128)} %packing_h.1, bf16[2,2,128,384]{3,2,1,0:T(8,128)(2,1)} %feat_h.1, f32[384]{0:T(512)} %gain_h.1, bf16[9,3,384,384]{3,2,1,0:T(8,128)(2,1)} %bitcast.2, f32[384]{0:T(512)} %cbias_h.1, ...), custom_call_target="tpu_custom_call" | custom-call | tf_op jit(solution)/shard_map/pallas_call | solution.py:464
  22.0 1.7 %shard_map.177 = (bf16[512,1280]{1,0:T(8,128)(2,1)}, bf16[512,1280]{1,0:T(8,128)(2,1)}) custom-call(bf16[512,256]{1,0:T(8,128)(2,1)S(1)} %get-tuple-element.5.left, f32[2,512,128]{2,1,0:T(8,128)S(1)} %get-tuple-element.6.coef, bf16[256,2560]{1,0:T(8,128)(2,1)S(1)} %get-tuple-element.7.mat), custom_call_target="tpu_custom_call" | custom-call | tf_op jit(solution)/shard_map/pallas_call | solution.py:503

commit v7 on v5

--- a/solution.py
+++ b/solution.py
@@ -49,7 +49,7 @@
     ]
     copies = [pltpu.make_async_copy(s, d, lsem.at[i]) for i, (s, d) in enumerate(early + late)]
     first, later = copies[: len(early)], copies[len(early) :]
-    runs = [(0, 2), (2, 2), (4, 2), (6, 2), (8, 1)]
+    runs = [(0, 1), (1, 2), (3, 2), (5, 2), (7, 2)]
     taps = [
         pltpu.make_async_copy(conv_h.at[pl.ds(i, n)], conv.at[pl.ds(i, n)], csem.at[k]) for k, (i, n) in enumerate(runs)
     ]
@@ -312,8 +312,12 @@
         lax.fori_loop(first, last, lambda i, c: (body(i), c)[1], 0)
 
     to_mate(group - 1).start()
-    loop(0, away, lambda i: spread(i).start())
-    loop(away, group - 1, lambda i: spread(i).start())
+    cuts = (0, min(flat, group - 1), min(2 * flat, group - 1), group - 1)
+
+    def release(k):
+        loop(cuts[k], cuts[k + 1], lambda i: spread(i).start())
+
+    release(0)
 
     def relay(j, skip):
         _, pr = place(j * flat)
@@ -321,7 +325,9 @@
         loop(j * flat, (j + 1) * flat - skip, lambda i: to_mate(i).start())
 
     lax.fori_loop(ahead, middle, both, 0)
+    release(1)
     shares = [share(0)]
+    release(2)
     lax.fori_loop(middle, count_n, both, 0)
     shares.append(share(1))
     for c in range(0, width, step):
@@ -335,8 +341,6 @@
     relay(outer - 1, 1)
     for j in range(outer - 2, -1, -1):
         relay(j, 0)
-    all_of(group, 1, outer).wait_recv()
-
     for h in range(2):
         gram_out[1 + h] = gram_s[h]
         shares[h].wait_recv()
@@ -345,40 +349,54 @@
 
     lane1 = lax.broadcasted_iota(jnp.int32, (1, 128), 1)
     hf = feats // 2
-    quads, ends = [], []
+    quads, tails = [], []
     for h in range(3):
         top, tail = gram_out[h, 0:hf, :], gram_out[h, hf : hf + 8, :]
         square = jnp.where(lane1 < feats, jnp.concatenate([top, pltpu.roll(top, feats, 1)], axis=0), 0.0)
         quads.append(square)
-        ends.append(jnp.where(lane1 < feats, tail, 0.0))
+        tails.append(jnp.where(lane1 < feats, tail, 0.0))
 
     def entry(h, row, at):
         return jnp.sum(jnp.where(lane1 == at, gram_out[h, hf + row : hf + row + 1, :], 0.0), axis=1, keepdims=True)
 
-    hi, lo = split(jnp.concatenate(quads + ends, axis=0))
+    hi, lo = split(jnp.concatenate(quads + tails, axis=0))
     lo_at = pltpu.roll(lo.astype(F32), feats, 1).astype(BF16)
     stacked = hi + lo_at
-    at16 = lax.broadcasted_iota(jnp.int32, (16, cols), 0)
+    var_end = entry(0, 0, feats)
+    ends = [(entry(h, 0, feats), entry(h, 0, feats + 1), entry(h, 1, feats + 1)) for h in (1, 2)]
+
+    all_of(group, 1, outer).wait_recv()
+
+    tokens = count_t * cols
+    xs = jnp.concatenate([lat_all[packing[r * count_t + j]] for j in range(count_t)], axis=1)
+    prod = dot(stacked, jnp.concatenate([xs, xs], axis=0))
+    x = xs.astype(F32)
+
+    def line(h, row):
+        return prod[3 * feats + 8 * h + row : 3 * feats + 8 * h + row + 1, :]
+
+    def square(h):
+        return jnp.sum(x * prod[h * feats : (h + 1) * feats, :], axis=0, keepdims=True)
+
+    var = (square(0) + 2.0 * line(0, 0) + var_end) / width + epsilon
+    inv = lax.rsqrt(var)
+    sigma = var * inv
+    high = sigma.astype(BF16).astype(F32)
+    mid = (sigma - high).astype(BF16).astype(F32)
+    at16 = lax.broadcasted_iota(jnp.int32, (16, tokens), 0)
+    more = jnp.where(at16 < 4, high, jnp.where(at16 < 6, mid, sigma - high - mid))
+    more = jnp.where(at16 < 2, 1.0, jnp.where(at16 < 8, more, 0.0))
+    scales = []
+    for h in range(1, 3):
+        e0, e1, e2 = ends[h - 1]
+        ss = inv * inv * (square(h) + 2.0 * line(h, 0) + e0) + 2.0 * inv * (line(h, 1) + e1) + e2
+        scales.append(lax.rsqrt(ss / width + epsilon) * inv)
+    rest = jnp.zeros((2 * feats - 16, cols), F32)
     for j in range(count_t):
-        x = lat_all[packing[r * count_t + j]]
-        prod = dot(stacked, jnp.concatenate([x, x], axis=0))
-        x = x.astype(F32)
-        line = lambda h, row: prod[3 * feats + 8 * h + row : 3 * feats + 8 * h + row + 1, :]
-        square = lambda h: jnp.sum(x * prod[h * feats : (h + 1) * feats, :], axis=0, keepdims=True)
-        var = (square(0) + 2.0 * line(0, 0) + entry(0, 0, feats)) / width + epsilon
-        inv = lax.rsqrt(var)
-        sigma = var * inv
-        high = sigma.astype(BF16).astype(F32)
-        mid = (sigma - high).astype(BF16).astype(F32)
-        more = jnp.where(at16 < 4, high, jnp.where(at16 < 6, mid, sigma - high - mid))
-        more = jnp.where(at16 < 2, 1.0, jnp.where(at16 < 8, more, 0.0))
-        at = pl.ds(j * cols, cols)
-        rest = jnp.zeros((2 * feats - 16, cols), F32)
-        left[at, :] = jnp.concatenate([x, x, more, rest], axis=0).T.astype(BF16)
-        for h in range(1, 3):
-            ss = inv * inv * (square(h) + 2.0 * line(h, 0) + entry(h, 0, feats))
-            ss = ss + 2.0 * inv * (line(h, 1) + entry(h, 0, feats + 1)) + entry(h, 1, feats + 1)
-            coef[h - 1, at, :] = jnp.broadcast_to(lax.rsqrt(ss / width + epsilon) * inv, (128, cols)).T
+        at = slice(j * cols, (j + 1) * cols)
+        left[at, :] = jnp.concatenate([x[:, at], x[:, at], more[:, at], rest], axis=0).T.astype(BF16)
+        for h in range(2):
+            coef[h, at, :] = jnp.broadcast_to(scales[h][:, at], (128, cols)).T
 
     for copy, p in zip(halo, plan):
         pl.when(p[4])(copy.wait_send)

time: 23.6 us -> 23.3 us (0.987)
  Pallas kernels: 22.9 us -> 22.5 us
    pallas_call x1, Pallas kernels: 21.1 us -> 20.8 us  [per_device(): pl.pallas_call(functools.partial(kernel, count_t, count_r), out_shape=out...]
where the time goes in v7:
time: 23.3 us; the launch traced here: 23.1 us
  Pallas kernels  22.5 us (97%)
  between operations  0.65 us (3%)
    pallas_call x1, Pallas kernels, per_device(): pl.pallas_call(functools.partial(kernel, count_t, count_r), out_shape=out...  20.8 us
    pallas_call x1, Pallas kernels, finish(): pl.pallas_call(final, out_shape=(out, out), in_specs=[pl.BlockSpec(memory...  1.73 us

profile of v7, /device:TPU:1, one launch (start us, length us, event | category | flops | bytes accessed | tf_op | source)
XLA Modules:
  0.0 23.1 jit_solution(13388036458971645927)
XLA Ops:
  0.6 20.8 %shard_map.176 = (bf16[512,256]{1,0:T(8,128)(2,1)S(1)}, f32[2,512,128]{2,1,0:T(8,128)S(1)}, bf16[256,2560]{1,0:T(8,128)(2,1)S(1)}) custom-call(s32[32]{0:T(128)} %packing_h.1, bf16[2,2,128,384]{3,2,1,0:T(8,128)(2,1)} %feat_h.1, f32[384]{0:T(512)} %gain_h.1, bf16[9,3,384,384]{3,2,1,0:T(8,128)(2,1)} %bitcast.2, f32[384]{0:T(512)} %cbias_h.1, ...), custom_call_target="tpu_custom_call" | custom-call | tf_op jit(solution)/shard_map/pallas_call | solution.py:462
  21.4 1.7 %shard_map.177 = (bf16[512,1280]{1,0:T(8,128)(2,1)}, bf16[512,1280]{1,0:T(8,128)(2,1)}) custom-call(bf16[512,256]{1,0:T(8,128)(2,1)S(1)} %get-tuple-element.5.left, f32[2,512,128]{2,1,0:T(8,128)S(1)} %get-tuple-element.6.coef, bf16[256,2560]{1,0:T(8,128)(2,1)S(1)} %get-tuple-element.7.mat), custom_call_target="tpu_custom_call" | custom-call | tf_op jit(solution)/shard_map/pallas_call | solution.py:501

commit v8 on v7

--- a/solution.py
+++ b/solution.py
@@ -145,8 +145,8 @@
             src_ref=snd.at[rows], dst_ref=rcv.at[rows], send_sem=hs_sem.at[k], recv_sem=hr_sem.at[k],
             device_id=(dt, dr), device_id_type=MESH,
         ))
-    for copy, p in zip(halo, plan):
-        pl.when(p[4])(copy.start)
+    for k in (3, 4, 0, 1, 2):
+        pl.when(plan[k][4])(halo[k].start)
 
     for c in later:
         c.wait()
@@ -311,13 +311,13 @@
     def loop(first, last, body):
         lax.fori_loop(first, last, lambda i, c: (body(i), c)[1], 0)
 
-    to_mate(group - 1).start()
     cuts = (0, min(flat, group - 1), min(2 * flat, group - 1), group - 1)
 
     def release(k):
         loop(cuts[k], cuts[k + 1], lambda i: spread(i).start())
 
     release(0)
+    to_mate(group - 1).start()
 
     def relay(j, skip):
         _, pr = place(j * flat)

time: 23.3 us -> 23.2 us (level)
  no operation moved by 1% of the time
where the time goes in v8:
time: 23.2 us; the launch traced here: 23 us
  Pallas kernels  22.4 us (97%)
  between operations  0.65 us (3%)
    pallas_call x1, Pallas kernels, per_device(): pl.pallas_call(functools.partial(kernel, count_t, count_r), out_shape=out...  20.7 us
    pallas_call x1, Pallas kernels, finish(): pl.pallas_call(final, out_shape=(out, out), in_specs=[pl.BlockSpec(memory...  1.73 us

profile of v8, /device:TPU:1, one launch (start us, length us, event | category | flops | bytes accessed | tf_op | source)
XLA Modules:
  0.0 23.0 jit_solution(131977159983042728)
XLA Ops:
  0.6 20.7 %shard_map.176 = (bf16[512,256]{1,0:T(8,128)(2,1)S(1)}, f32[2,512,128]{2,1,0:T(8,128)S(1)}, bf16[256,2560]{1,0:T(8,128)(2,1)S(1)}) custom-call(s32[32]{0:T(128)} %packing_h.1, bf16[2,2,128,384]{3,2,1,0:T(8,128)(2,1)} %feat_h.1, f32[384]{0:T(512)} %gain_h.1, bf16[9,3,384,384]{3,2,1,0:T(8,128)(2,1)} %bitcast.2, f32[384]{0:T(512)} %cbias_h.1, ...), custom_call_target="tpu_custom_call" | custom-call | tf_op jit(solution)/shard_map/pallas_call | solution.py:462
  21.3 1.7 %shard_map.177 = (bf16[512,1280]{1,0:T(8,128)(2,1)}, bf16[512,1280]{1,0:T(8,128)(2,1)}) custom-call(bf16[512,256]{1,0:T(8,128)(2,1)S(1)} %get-tuple-element.5.left, f32[2,512,128]{2,1,0:T(8,128)S(1)} %get-tuple-element.6.coef, bf16[256,2560]{1,0:T(8,128)(2,1)S(1)} %get-tuple-element.7.mat), custom_call_target="tpu_custom_call" | custom-call | tf_op jit(solution)/shard_map/pallas_call | solution.py:501
